TPU v7x, 512 devices: a whole 4x4x16 slice. The times are simulated.
512 devices in a mesh: leaf: 256 (over z, y, x), blk: 2 (over core).
Axes of the slice: x: 4, y: 4, z: 16, core: 2. Of those that a mesh axis runs over, the one named last changes fastest.
Arguments:
- obs_rows: bfloat16 [131072, 512], P('leaf'), may hold values from -0.25 to 0.25
- obs_values: float32 [131072], P('leaf'), may hold values from -24 to 24
- track_blocks: int32 [256], P('leaf'), may hold values from 1 to 4, as said below
- pattern: int32 [1024, 64], P('leaf'), may hold values 0 or 1
- process_info: float32 [512, 512], replicated, as said below
Outputs:
- leaf_mean: float32 [256, 512], P('leaf')
- leaf_cov: float32 [131072, 512], P('leaf', 'blk')
Inputs may be any that keep to these rules, and one draw needn't show every extreme that they name: `track_blocks`: some leaf has exactly 4 live row blocks in every draw; the others have 1 to 3. `process_info`: symmetric positive definite.
All inputs are finite; a program needn't handle non-finite values. No bound on the sum of `pattern` on one device may be relied on, other than what follows from the above.
Results may differ from a plain program's by a relative error of at most 0.0003.
Values sent between devices are 32-bit elements; how exact they have to be, the bound alone decides.
A program may use at most 128 MiB of HBM per device.

v0:
```python
import jax
import jax.numpy as jnp
from jax import lax
from jax.sharding import PartitionSpec as P

highest = lax.Precision.HIGHEST


def from_partner(value, axis, bit):
    mask = 2**bit
    pairs = [(source, source ^ mask) for source in range(lax.axis_size(axis))]
    return lax.ppermute(value, axis, pairs)


def copy_for_each(shard, axis):
    copies = jnp.broadcast_to(shard, (lax.axis_size(axis), *shard.shape))
    return lax.all_to_all(copies, axis, split_axis=0, concat_axis=0, tiled=True)


def laid_out(parts, dim):
    dims = list(parts.shape[1:])
    dims[dim] *= parts.shape[0]
    return jnp.moveaxis(parts, 0, dim).reshape(dims)


def gathered_copies(shard, axis, dim):
    parts = copy_for_each(shard, axis)
    return laid_out(parts, dim)


def product(left, right):
    return jnp.dot(left, right, precision=highest, preferred_element_type=jnp.float32)


def invert_factor(matrix_full):
    factor = jnp.linalg.cholesky(matrix_full)
    identity = jnp.eye(matrix_full.shape[0], dtype=jnp.float32)
    return jax.scipy.linalg.solve_triangular(factor, identity, lower=True)


def apply_inverse(inverse_factor, right):
    return product(inverse_factor.T, product(inverse_factor, right))


def trade(column_piece, vector, bit_index):
    return from_partner((column_piece, vector), "leaf", bit_index)


def shards(obs_rows, obs_values, track_blocks, pattern, process_info):
    states = process_info.shape[0]
    half_cols = states // 2
    core_index = lax.axis_index("blk")
    levels = (lax.axis_size("leaf").bit_length() - 1) // 2
    cap_blocks = pattern.shape[0]
    block_rows = obs_rows.shape[0] // cap_blocks
    block_width = states // pattern.shape[1]
    col_start = core_index * half_cols
    keep_mask = jnp.repeat(pattern.astype(jnp.bfloat16), block_width, axis=1)
    alive_mask = (jnp.arange(cap_blocks) < track_blocks[0]).astype(jnp.bfloat16)
    keep_mask = keep_mask * alive_mask[:, None]
    masked_rows = obs_rows.reshape(cap_blocks, block_rows, states) * keep_mask[:, None, :]
    own_cols = lax.dynamic_slice_in_dim(masked_rows, col_start, half_cols, 2)
    info_cur = jnp.einsum("brs,brc->sc", masked_rows, own_cols, preferred_element_type=jnp.float32)
    flat_rows = masked_rows.reshape(-1, states)
    vec_cur = jnp.dot(obs_values, flat_rows, precision=highest, preferred_element_type=jnp.float32)
    proc_cols = lax.dynamic_slice_in_dim(process_info, col_start, half_cols, 1)
    eye_cols = (jnp.arange(states)[:, None] == col_start + jnp.arange(half_cols)[None, :]).astype(
        jnp.float32
    )
    stored = []
    for tier_index in range(levels + 1):
        matrix_part = info_cur + proc_cols
        matrix_full = gathered_copies(matrix_part, "blk", 1)
        inverse_factor = invert_factor(matrix_full)
        if tier_index == levels:
            stored.append((inverse_factor, vec_cur, proc_cols))
        else:
            msg_vec = product(process_info, apply_inverse(inverse_factor, vec_cur))
            gain_part = apply_inverse(inverse_factor, proc_cols)
            msg_part = proc_cols - product(process_info, gain_part)
            stored.append((inverse_factor, vec_cur, gain_part))
            info_cur, vec_cur = (msg_part, msg_vec)
            for bit_index in (2 * tier_index, 2 * tier_index + 1):
                partner = trade(info_cur, vec_cur, bit_index)
                info_cur = info_cur + partner[0]
                vec_cur = vec_cur + partner[1]
    root_inverse, root_vec, unused_gain = stored[levels]
    mean_vec = apply_inverse(root_inverse, root_vec)
    cov_part = apply_inverse(root_inverse, eye_cols)
    for tier_index in range(levels - 1, -1, -1):
        inverse_factor, vec_node, gain_part = stored[tier_index]
        own_inverse = lax.dynamic_slice_in_dim(inverse_factor, col_start, half_cols, 1)
        inverse_cols = product(inverse_factor.T, own_inverse)
        gain_rows = product(inverse_cols.T, process_info)
        cov_full = gathered_copies(cov_part, "blk", 1)
        inner_prod = lax.dot_general(
            cov_full,
            gain_rows,
            (((1,), (1,)), ((), ())),
            precision=highest,
            preferred_element_type=jnp.float32,
        )
        cov_part = apply_inverse(inverse_factor, eye_cols + product(process_info, inner_prod))
        mean_vec = apply_inverse(inverse_factor, vec_node + product(process_info, mean_vec))
    return (mean_vec[None, :], cov_part)


def solution(mesh):
    placed = (P("leaf", None), P("leaf"), P("leaf"), P("leaf", None), P())
    return jax.shard_map(
        shards,
        mesh=mesh,
        in_specs=placed,
        out_specs=(P("leaf", None), P("leaf", "blk")),
        check_vma=False,
    )
```

profile of v0, /device:TPU:1, one launch (start us, length us, event | category | flops | bytes accessed | tf_op | source)
XLA Modules:
  0.0 1104.9 jit_solution(15608670852774591580)
XLA Ops:
  5.2 10.4 all-to-all-start
  21.0 11.7 %cholesky.550 = f32[128,128]{1,0:T(8,128)S(1)} custom-call(f32[128,128]{1,0:T(8,128)S(1)} %cholesky.906), custom_call_target="Cholesky" | custom-call | tf_op jit(solution)/shard_map/jit(cholesky)/cholesky | solution.py:36
  32.9 9.8 custom-call.39
  45.9 11.7 %cholesky.569 = f32[128,128]{1,0:T(8,128)S(1)} custom-call(f32[128,128]{1,0:T(8,128)S(1)} %cholesky.910), custom_call_target="Cholesky" | custom-call | tf_op jit(solution)/shard_map/jit(cholesky)/cholesky | solution.py:36
  57.7 10.2 custom-call.40
  69.5 11.7 %cholesky.590 = f32[128,128]{1,0:T(8,128)S(1)} custom-call(f32[128,128]{1,0:T(8,128)S(1)} %cholesky.915), custom_call_target="Cholesky" | custom-call | tf_op jit(solution)/shard_map/jit(cholesky)/cholesky | solution.py:36
  81.3 9.8 custom-call.41
  92.5 11.7 %cholesky.607 = f32[128,128]{1,0:T(8,128)S(1)} custom-call(f32[128,128]{1,0:T(8,128)S(1)} %convolution_subtract_fusion.29), custom_call_target="Cholesky" | custom-call | tf_op jit(solution)/shard_map/jit(cholesky)/cholesky | solution.py:36
  110.1 12.0 %while.10 = (s32[]{:T(128)}, f32[512,512]{1,0:T(8,128)}, s32[4,2]{0,1:T(2,128)S(1)}, f32[4,128,128]{2,1,0:T(8,128)S(1)}, s32[]{:T(128)}) while((s32[]{:T(128)}, f32[512,512]{1,0:T(8,128)}, s32[4,2]{0,1:T(2,128)S(1)}, f32[4,128,128]{2,1,0:T(8,128)S(1)}, s32[]{:T(128)}) %tuple.118), condition=%wide.while_cond, body=%wide.while_body.sunk | while | flops 2 | bytes 131189 | solution.py:38
  122.2 39.3 %custom-call.42 = f32[4,128,128]{1,2,0:T(8,128)S(1)} custom-call(f32[4,128,128]{2,1,0:T(8,128)S(1)} %get-tuple-element.36), custom_call_target="InvertDiagBlocksLowerTriangular" | custom-call | tf_op jit(solution)/shard_map/jit(_solve_triangular)/triangular_solve | solution.py:38
  179.9 6.6 collective-permute-done
  192.3 4.9 collective-permute-start.3
  197.1 5.2 collective-permute-done.3
  204.5 6.2 all_to_all.45
  214.4 11.7 %cholesky.622 = f32[128,128]{1,0:T(8,128)S(1)} custom-call(f32[128,128]{1,0:T(8,128)S(1)} %cholesky.919), custom_call_target="Cholesky" | custom-call | tf_op jit(solution)/shard_map/jit(cholesky)/cholesky | solution.py:36
  226.3 9.8 custom-call.43
  239.3 11.7 %cholesky.641 = f32[128,128]{1,0:T(8,128)S(1)} custom-call(f32[128,128]{1,0:T(8,128)S(1)} %cholesky.923), custom_call_target="Cholesky" | custom-call | tf_op jit(solution)/shard_map/jit(cholesky)/cholesky | solution.py:36
  251.7 9.9 custom-call.44
  264.7 13.2 %cholesky.662 = f32[128,128]{1,0:T(8,128)} custom-call(f32[128,128]{1,0:T(8,128)} %cholesky.928), custom_call_target="Cholesky" | custom-call | tf_op jit(solution)/shard_map/jit(cholesky)/cholesky | solution.py:36
  279.9 11.3 %custom-call.45 = f32[1,128,128]{1,2,0:T(8,128)} custom-call(f32[1,128,128]{2,1,0:T(8,128)} %get-tuple-element.124), custom_call_target="InvertDiagBlocksLowerTriangular" | custom-call | tf_op jit(solution)/shard_map/jit(cholesky)/cholesky | solution.py:36
  293.4 11.7 %cholesky.679 = f32[128,128]{1,0:T(8,128)S(1)} custom-call(f32[128,128]{1,0:T(8,128)S(1)} %convolution_subtract_fusion.28), custom_call_target="Cholesky" | custom-call | tf_op jit(solution)/shard_map/jit(cholesky)/cholesky | solution.py:36
  313.3 11.5 %while.11 = (s32[]{:T(128)}, f32[512,512]{1,0:T(8,128)}, s32[4,2]{0,1:T(2,128)S(1)}, f32[4,128,128]{2,1,0:T(8,128)S(1)}, s32[]{:T(128)}) while((s32[]{:T(128)}, f32[512,512]{1,0:T(8,128)}, s32[4,2]{0,1:T(2,128)S(1)}, f32[4,128,128]{2,1,0:T(8,128)S(1)}, s32[]{:T(128)}) %tuple.133), condition=%wide.while_cond.clone, body=%wide.while_body.clone.sunk | while | flops 2 | bytes 131189 | solution.py:38
  324.8 39.3 %custom-call.46 = f32[4,128,128]{1,2,0:T(8,128)S(1)} custom-call(f32[4,128,128]{2,1,0:T(8,128)S(1)} %get-tuple-element.37), custom_call_target="InvertDiagBlocksLowerTriangular" | custom-call | tf_op jit(solution)/shard_map/jit(_solve_triangular)/triangular_solve | solution.py:38
  382.2 8.0 collective-permute-done.4
  394.0 4.9 collective-permute-start.7
  400.8 5.1 collective-permute-done.7
  407.0 6.3 all_to_all.46
  416.9 11.7 %cholesky.694 = f32[128,128]{1,0:T(8,128)S(1)} custom-call(f32[128,128]{1,0:T(8,128)S(1)} %cholesky.932), custom_call_target="Cholesky" | custom-call | tf_op jit(solution)/shard_map/jit(cholesky)/cholesky | solution.py:36
  428.8 9.8 custom-call.47
  441.8 11.7 %cholesky.713 = f32[128,128]{1,0:T(8,128)S(1)} custom-call(f32[128,128]{1,0:T(8,128)S(1)} %cholesky.936), custom_call_target="Cholesky" | custom-call | tf_op jit(solution)/shard_map/jit(cholesky)/cholesky | solution.py:36
  454.2 10.2 custom-call.48
  467.4 13.2 %cholesky.734 = f32[128,128]{1,0:T(8,128)} custom-call(f32[128,128]{1,0:T(8,128)} %cholesky.941), custom_call_target="Cholesky" | custom-call | tf_op jit(solution)/shard_map/jit(cholesky)/cholesky | solution.py:36
  482.6 11.3 %custom-call.49 = f32[1,128,128]{1,2,0:T(8,128)} custom-call(f32[1,128,128]{2,1,0:T(8,128)} %get-tuple-element.114), custom_call_target="InvertDiagBlocksLowerTriangular" | custom-call | tf_op jit(solution)/shard_map/jit(cholesky)/cholesky | solution.py:36
  496.2 11.7 %cholesky.751 = f32[128,128]{1,0:T(8,128)S(1)} custom-call(f32[128,128]{1,0:T(8,128)S(1)} %convolution_subtract_fusion.27), custom_call_target="Cholesky" | custom-call | tf_op jit(solution)/shard_map/jit(cholesky)/cholesky | solution.py:36
  515.6 11.5 %while.12 = (s32[]{:T(128)}, f32[512,512]{1,0:T(8,128)}, s32[4,2]{0,1:T(2,128)S(1)}, f32[4,128,128]{2,1,0:T(8,128)S(1)}, s32[]{:T(128)}) while((s32[]{:T(128)}, f32[512,512]{1,0:T(8,128)}, s32[4,2]{0,1:T(2,128)S(1)}, f32[4,128,128]{2,1,0:T(8,128)S(1)}, s32[]{:T(128)}) %tuple.134), condition=%wide.while_cond.clone.1, body=%wide.while_body.clone.1.sunk | while | flops 2 | bytes 131189 | solution.py:38
  527.0 39.3 %custom-call.50 = f32[4,128,128]{1,2,0:T(8,128)S(1)} custom-call(f32[4,128,128]{2,1,0:T(8,128)S(1)} %get-tuple-element.38), custom_call_target="InvertDiagBlocksLowerTriangular" | custom-call | tf_op jit(solution)/shard_map/jit(_solve_triangular)/triangular_solve | solution.py:38
  584.4 8.0 collective-permute-done.8
  602.4 18.0 %collective-permute-done.11 = f32[512]{0:T(512)S(1)} collective-permute-done((f32[512]{0:T(512)S(1)}, f32[512]{0:T(512)S(1)}, u32[]{:S(2)}, u32[]{:S(2)}) %collective-permute-start.11) | collective-permute-done | bytes 2080 | tf_op jit(solution)/shard_map/ppermute | solution.py:12
  629.8 11.7 %cholesky.766 = f32[128,128]{1,0:T(8,128)S(1)} custom-call(f32[128,128]{1,0:T(8,128)S(1)} %cholesky.945), custom_call_target="Cholesky" | custom-call | tf_op jit(solution)/shard_map/jit(cholesky)/cholesky | solution.py:36
  641.7 9.8 custom-call.51
  654.7 11.7 %cholesky.785 = f32[128,128]{1,0:T(8,128)S(1)} custom-call(f32[128,128]{1,0:T(8,128)S(1)} %cholesky.949), custom_call_target="Cholesky" | custom-call | tf_op jit(solution)/shard_map/jit(cholesky)/cholesky | solution.py:36
  667.1 9.9 custom-call.52
  680.1 13.2 %cholesky.806 = f32[128,128]{1,0:T(8,128)} custom-call(f32[128,128]{1,0:T(8,128)} %cholesky.954), custom_call_target="Cholesky" | custom-call | tf_op jit(solution)/shard_map/jit(cholesky)/cholesky | solution.py:36
  695.3 11.3 %custom-call.53 = f32[1,128,128]{1,2,0:T(8,128)} custom-call(f32[1,128,128]{2,1,0:T(8,128)} %get-tuple-element.104), custom_call_target="InvertDiagBlocksLowerTriangular" | custom-call | tf_op jit(solution)/shard_map/jit(cholesky)/cholesky | solution.py:36
  708.9 11.7 %cholesky.823 = f32[128,128]{1,0:T(8,128)S(1)} custom-call(f32[128,128]{1,0:T(8,128)S(1)} %convolution_subtract_fusion.26), custom_call_target="Cholesky" | custom-call | tf_op jit(solution)/shard_map/jit(cholesky)/cholesky | solution.py:36
  728.5 11.2 %while.13 = (s32[]{:T(128)}, f32[512,512]{1,0:T(8,128)}, s32[4,2]{0,1:T(2,128)S(1)}, f32[4,128,128]{2,1,0:T(8,128)S(1)}, s32[]{:T(128)}) while((s32[]{:T(128)}, f32[512,512]{1,0:T(8,128)}, s32[4,2]{0,1:T(2,128)S(1)}, f32[4,128,128]{2,1,0:T(8,128)S(1)}, s32[]{:T(128)}) %tuple.135), condition=%wide.while_cond.clone.2, body=%wide.while_body.clone.2.sunk | while | flops 2 | bytes 131189 | solution.py:38
  739.6 39.3 %custom-call.54 = f32[4,128,128]{1,2,0:T(8,128)S(1)} custom-call(f32[4,128,128]{2,1,0:T(8,128)S(1)} %get-tuple-element.39), custom_call_target="InvertDiagBlocksLowerTriangular" | custom-call | tf_op jit(solution)/shard_map/jit(_solve_triangular)/triangular_solve | solution.py:38
  796.1 4.7 collective-permute-start.14
  800.9 39.9 %collective-permute-done.12 = f32[512,256]{1,0:T(8,128)S(1)} collective-permute-done((f32[512,256]{1,0:T(8,128)S(1)}, f32[512,256]{1,0:T(8,128)S(1)}, u32[]{:S(2)}, u32[]{:S(2)}) %collective-permute-start.12) | collective-permute-done | bytes 524320 | tf_op jit(solution)/shard_map/ppermute | solution.py:12
  840.9 22.7 %collective-permute-start.13 = (f32[512,256]{1,0:T(8,128)S(1)}, f32[512,256]{1,0:T(8,128)S(1)}, u32[]{:S(2)}, u32[]{:S(2)}) collective-permute-start(f32[512,256]{1,0:T(8,128)S(1)} %add.155), channel_id=1, source_target_pairs={{0,256},{2,258},{4,260},{6,262},{8,264},{10,266},{12,268},{14,270}... | collective-permute-start | bytes 1572872 | tf_op jit(solution)/shard_map/ppermute | solution.py:12
  869.2 13.0 %collective-permute-done.15 = f32[512]{0:T(512)S(1)} collective-permute-done((f32[512]{0:T(512)S(1)}, f32[512]{0:T(512)S(1)}, u32[]{:S(2)}, u32[]{:S(2)}) %collective-permute-start.15) | collective-permute-done | bytes 2080 | tf_op jit(solution)/shard_map/ppermute | solution.py:12
  891.7 11.7 %cholesky.838 = f32[128,128]{1,0:T(8,128)S(1)} custom-call(f32[128,128]{1,0:T(8,128)S(1)} %cholesky.958), custom_call_target="Cholesky" | custom-call | tf_op jit(solution)/shard_map/jit(cholesky)/cholesky | solution.py:36
  903.6 9.8 custom-call.55
  916.6 11.7 %cholesky.857 = f32[128,128]{1,0:T(8,128)S(1)} custom-call(f32[128,128]{1,0:T(8,128)S(1)} %cholesky.962), custom_call_target="Cholesky" | custom-call | tf_op jit(solution)/shard_map/jit(cholesky)/cholesky | solution.py:36
  928.9 10.2 custom-call.56
  942.2 13.2 %cholesky.878 = f32[128,128]{1,0:T(8,128)} custom-call(f32[128,128]{1,0:T(8,128)} %cholesky.967), custom_call_target="Cholesky" | custom-call | tf_op jit(solution)/shard_map/jit(cholesky)/cholesky | solution.py:36
  957.4 11.3 %custom-call.57 = f32[1,128,128]{1,2,0:T(8,128)} custom-call(f32[1,128,128]{2,1,0:T(8,128)} %get-tuple-element.94), custom_call_target="InvertDiagBlocksLowerTriangular" | custom-call | tf_op jit(solution)/shard_map/jit(cholesky)/cholesky | solution.py:36
  970.9 11.7 %cholesky.895 = f32[128,128]{1,0:T(8,128)S(1)} custom-call(f32[128,128]{1,0:T(8,128)S(1)} %convolution_subtract_fusion.25), custom_call_target="Cholesky" | custom-call | tf_op jit(solution)/shard_map/jit(cholesky)/cholesky | solution.py:36
  990.7 11.6 %while.14 = (s32[]{:T(128)}, f32[512,512]{1,0:T(8,128)}, s32[4,2]{0,1:T(2,128)S(1)}, f32[4,128,128]{2,1,0:T(8,128)S(1)}, s32[]{:T(128)}) while((s32[]{:T(128)}, f32[512,512]{1,0:T(8,128)}, s32[4,2]{0,1:T(2,128)S(1)}, f32[4,128,128]{2,1,0:T(8,128)S(1)}, s32[]{:T(128)}) %tuple.136), condition=%wide.while_cond.clone.3, body=%wide.while_body.clone.3.sunk | while | flops 2 | bytes 131189 | solution.py:38
  1002.3 39.3 %custom-call.58 = f32[4,128,128]{1,2,0:T(8,128)S(1)} custom-call(f32[4,128,128]{2,1,0:T(8,128)S(1)} %get-tuple-element.40), custom_call_target="InvertDiagBlocksLowerTriangular" | custom-call | tf_op jit(solution)/shard_map/jit(_solve_triangular)/triangular_solve | solution.py:38
  1063.6 4.7 all_to_all.49
  1073.5 4.7 all_to_all.50
  1083.4 4.9 all_to_all.51
  1093.5 4.7 all_to_all.52
  (470 shorter events, 314.4 us)
Async XLA Ops:
  0.6 172.8 %copy-start = (f32[512]{0:T(512)S(1)}, f32[512]{0:T(512)}, u32[]{:S(2)}) copy-start(f32[512]{0:T(512)} %param.9) | copy-start | bytes 6148
  0.6 2.9 copy-start.2
  5.2 12.1 %all-to-all-start = ((f32[2,512,256]{1,2,0:T(8,128)}), f32[2,512,256]{1,2,0:T(8,128)S(1)}, u32[]{:S(2)}, u32[]{:S(2)}) async-start(f32[2,512,256]{1,2,0:T(8,128)} %broadcast_in_dim.39), calls=%async_computation | async-start | bytes 2097152 | tf_op jit(solution)/shard_map/all_to_all | solution.py:17
  20.0 1.0 copy-start.17
  45.9 22.0 %copy-start.44 = (f32[384,128]{1,0:T(8,128)S(1)}, f32[384,128]{1,0:T(8,128)}, u32[]{:S(2)}) copy-start(f32[384,128]{1,0:T(8,128)} %copy-done.43) | copy-start | bytes 589828
  163.6 16.2 %copy-start.9 = (f32[128,512]{1,0:T(8,128)}, f32[128,512]{1,0:T(8,128)S(1)}, u32[]{:S(2)}) copy-start(f32[128,512]{1,0:T(8,128)S(1)} %fusion.161) | copy-start | bytes 786436
  165.4 14.3 %copy-start.22 = (f32[128,512]{1,0:T(8,128)}, f32[128,512]{1,0:T(8,128)S(1)}, u32[]{:S(2)}) copy-start(f32[128,512]{1,0:T(8,128)S(1)} %fusion.159) | copy-start | bytes 786436
  167.5 12.3 %copy-start.35 = (f32[128,512]{1,0:T(8,128)}, f32[128,512]{1,0:T(8,128)S(1)}, u32[]{:S(2)}) copy-start(f32[128,512]{1,0:T(8,128)S(1)} %fusion.158) | copy-start | bytes 786436
  170.4 3.0 copy-start.30
  171.5 15.0 %collective-permute-start = (f32[512,256]{1,0:T(8,128)S(1)}, f32[512,256]{1,0:T(8,128)S(1)}, u32[]{:S(2)}, u32[]{:S(2)}) collective-permute-start(f32[512,256]{1,0:T(8,128)S(1)} %fusion.7), channel_id=1, source_target_pairs={{0,2},{2,0},{4,6},{6,4},{8,10},{10,8},{12,14},{14,12},{16,18},{18,... | collective-permute-start | bytes 1572872 | tf_op jit(solution)/shard_map/ppermute | solution.py:12
  176.4 15.9 %collective-permute-start.2 = (f32[512]{0:T(512)S(1)}, f32[512]{0:T(512)S(1)}, u32[]{:S(2)}, u32[]{:S(2)}) collective-permute-start(f32[512]{0:T(512)S(1)} %bitcast.506), channel_id=1, source_target_pairs={{0,2},{2,0},{4,6},{6,4},{8,10},{10,8},{12,14},{14,12},{16,18},{18,... | collective-permute-start | bytes 6152 | tf_op jit(solution)/shard_map/ppermute | solution.py:12
  186.6 16.4 %collective-permute-start.1 = (f32[512,256]{1,0:T(8,128)S(1)}, f32[512,256]{1,0:T(8,128)}, u32[]{:S(2)}, u32[]{:S(2)}) collective-permute-start(f32[512,256]{1,0:T(8,128)S(1)} %add.140), channel_id=1, source_target_pairs={{0,4},{2,6},{4,0},{6,2},{8,12},{10,14},{12,8},{14,10},{16,20},{18,... | collective-permute-start | bytes 1572872 | tf_op jit(solution)/shard_map/ppermute | solution.py:12
  192.3 10.1 collective-permute-start.3
  364.6 17.5 %copy-start.3 = (f32[128,512]{1,0:T(8,128)}, f32[128,512]{1,0:T(8,128)S(1)}, u32[]{:S(2)}) copy-start(f32[128,512]{1,0:T(8,128)S(1)} %fusion.87) | copy-start | bytes 786436
  366.3 15.8 %copy-start.11 = (f32[128,512]{1,0:T(8,128)}, f32[128,512]{1,0:T(8,128)S(1)}, u32[]{:S(2)}) copy-start(f32[128,512]{1,0:T(8,128)S(1)} %fusion.155) | copy-start | bytes 786436
  368.2 13.9 %copy-start.24 = (f32[128,512]{1,0:T(8,128)}, f32[128,512]{1,0:T(8,128)S(1)}, u32[]{:S(2)}) copy-start(f32[128,512]{1,0:T(8,128)S(1)} %fusion.153) | copy-start | bytes 786436
  370.3 11.8 %copy-start.37 = (f32[128,512]{1,0:T(8,128)}, f32[128,512]{1,0:T(8,128)S(1)}, u32[]{:S(2)}) copy-start(f32[128,512]{1,0:T(8,128)S(1)} %fusion.152) | copy-start | bytes 786436
  370.3 1.0 copy-start.49
  375.1 15.0 %collective-permute-start.4 = (f32[512,256]{1,0:T(8,128)S(1)}, f32[512,256]{1,0:T(8,128)S(1)}, u32[]{:S(2)}, u32[]{:S(2)}) collective-permute-start(f32[512,256]{1,0:T(8,128)S(1)} %fusion.6), channel_id=1, source_target_pairs={{0,8},{2,10},{4,12},{6,14},{8,0},{10,2},{12,4},{14,6},{16,24},{18,... | collective-permute-start | bytes 1572872 | tf_op jit(solution)/shard_map/ppermute | solution.py:12
  378.7 15.3 %collective-permute-start.6 = (f32[512]{0:T(512)S(1)}, f32[512]{0:T(512)S(1)}, u32[]{:S(2)}, u32[]{:S(2)}) collective-permute-start(f32[512]{0:T(512)S(1)} %bitcast.508), channel_id=1, source_target_pairs={{0,8},{2,10},{4,12},{6,14},{8,0},{10,2},{12,4},{14,6},{16,24},{18,... | collective-permute-start | bytes 6152 | tf_op jit(solution)/shard_map/ppermute | solution.py:12
  390.2 16.3 %collective-permute-start.5 = (f32[512,256]{1,0:T(8,128)S(1)}, f32[512,256]{1,0:T(8,128)S(1)}, u32[]{:S(2)}, u32[]{:S(2)}) collective-permute-start(f32[512,256]{1,0:T(8,128)S(1)} %add.145), channel_id=1, source_target_pairs={{0,16},{2,18},{4,20},{6,22},{8,24},{10,26},{12,28},{14,30},{16,0},... | collective-permute-start | bytes 1572872 | tf_op jit(solution)/shard_map/ppermute | solution.py:12
  394.0 11.9 %collective-permute-start.7 = (f32[512]{0:T(512)S(1)}, f32[512]{0:T(512)S(1)}, u32[]{:S(2)}, u32[]{:S(2)}) collective-permute-start(f32[512]{0:T(512)S(1)} %add.148), channel_id=1, source_target_pairs={{0,16},{2,18},{4,20},{6,22},{8,24},{10,26},{12,28},{14,30},{16,0},... | collective-permute-start | bytes 6152 | tf_op jit(solution)/shard_map/ppermute | solution.py:12
  566.8 17.5 %copy-start.5 = (f32[128,512]{1,0:T(8,128)}, f32[128,512]{1,0:T(8,128)S(1)}, u32[]{:S(2)}) copy-start(f32[128,512]{1,0:T(8,128)S(1)} %fusion.85) | copy-start | bytes 786436
  568.5 15.8 %copy-start.13 = (f32[128,512]{1,0:T(8,128)}, f32[128,512]{1,0:T(8,128)S(1)}, u32[]{:S(2)}) copy-start(f32[128,512]{1,0:T(8,128)S(1)} %fusion.149) | copy-start | bytes 786436
  570.4 13.9 %copy-start.26 = (f32[128,512]{1,0:T(8,128)}, f32[128,512]{1,0:T(8,128)S(1)}, u32[]{:S(2)}) copy-start(f32[128,512]{1,0:T(8,128)S(1)} %fusion.147) | copy-start | bytes 786436
  572.5 11.8 %copy-start.39 = (f32[128,512]{1,0:T(8,128)}, f32[128,512]{1,0:T(8,128)S(1)}, u32[]{:S(2)}) copy-start(f32[128,512]{1,0:T(8,128)S(1)} %fusion.146) | copy-start | bytes 786436
  572.5 1.0 copy-start.51
  577.4 15.0 %collective-permute-start.8 = (f32[512,256]{1,0:T(8,128)S(1)}, f32[512,256]{1,0:T(8,128)S(1)}, u32[]{:S(2)}, u32[]{:S(2)}) collective-permute-start(f32[512,256]{1,0:T(8,128)S(1)} %fusion.5), channel_id=1, source_target_pairs={{0,32},{2,34},{4,36},{6,38},{8,40},{10,42},{12,44},{14,46},{16,48}... | collective-permute-start | bytes 1572872 | tf_op jit(solution)/shard_map/ppermute | solution.py:12
  580.9 15.3 %collective-permute-start.10 = (f32[512]{0:T(512)S(1)}, f32[512]{0:T(512)S(1)}, u32[]{:S(2)}, u32[]{:S(2)}) collective-permute-start(f32[512]{0:T(512)S(1)} %bitcast.510), channel_id=1, source_target_pairs={{0,32},{2,34},{4,36},{6,38},{8,40},{10,42},{12,44},{14,46},{16,48}... | collective-permute-start | bytes 6152 | tf_op jit(solution)/shard_map/ppermute | solution.py:12
  592.5 28.5 %collective-permute-start.9 = (f32[512,256]{1,0:T(8,128)S(1)}, f32[512,256]{1,0:T(8,128)S(1)}, u32[]{:S(2)}, u32[]{:S(2)}) collective-permute-start(f32[512,256]{1,0:T(8,128)S(1)} %add.150), channel_id=1, source_target_pairs={{0,64},{2,66},{4,68},{6,70},{8,72},{10,74},{12,76},{14,78},{16,80}... | collective-permute-start | bytes 1572872 | tf_op jit(solution)/shard_map/ppermute | solution.py:12
  596.2 24.2 %collective-permute-start.11 = (f32[512]{0:T(512)S(1)}, f32[512]{0:T(512)S(1)}, u32[]{:S(2)}, u32[]{:S(2)}) collective-permute-start(f32[512]{0:T(512)S(1)} %add.153), channel_id=1, source_target_pairs={{0,64},{2,66},{4,68},{6,70},{8,72},{10,74},{12,76},{14,78},{16,80}... | collective-permute-start | bytes 6152 | tf_op jit(solution)/shard_map/ppermute | solution.py:12
  779.4 21.4 %copy-start.7 = (f32[128,512]{1,0:T(8,128)}, f32[128,512]{1,0:T(8,128)S(1)}, u32[]{:S(2)}) copy-start(f32[128,512]{1,0:T(8,128)S(1)} %fusion.83) | copy-start | bytes 786436
  781.1 19.7 %copy-start.15 = (f32[128,512]{1,0:T(8,128)}, f32[128,512]{1,0:T(8,128)S(1)}, u32[]{:S(2)}) copy-start(f32[128,512]{1,0:T(8,128)S(1)} %fusion.143) | copy-start | bytes 786436
  783.0 17.8 %copy-start.28 = (f32[128,512]{1,0:T(8,128)}, f32[128,512]{1,0:T(8,128)S(1)}, u32[]{:S(2)}) copy-start(f32[128,512]{1,0:T(8,128)S(1)} %fusion.141) | copy-start | bytes 786436
  785.1 15.8 %copy-start.41 = (f32[128,512]{1,0:T(8,128)}, f32[128,512]{1,0:T(8,128)S(1)}, u32[]{:S(2)}) copy-start(f32[128,512]{1,0:T(8,128)S(1)} %fusion.140) | copy-start | bytes 786436
  785.1 1.0 copy-start.53
  790.0 50.9 %collective-permute-start.12 = (f32[512,256]{1,0:T(8,128)S(1)}, f32[512,256]{1,0:T(8,128)S(1)}, u32[]{:S(2)}, u32[]{:S(2)}) collective-permute-start(f32[512,256]{1,0:T(8,128)S(1)} %fusion.4), channel_id=1, source_target_pairs={{0,128},{2,130},{4,132},{6,134},{8,136},{10,138},{12,140},{14,142}... | collective-permute-start | bytes 1572872 | tf_op jit(solution)/shard_map/ppermute | solution.py:12
  796.1 69.3 %collective-permute-start.14 = (f32[512]{0:T(512)S(1)}, f32[512]{0:T(512)S(1)}, u32[]{:S(2)}, u32[]{:S(2)}) collective-permute-start(f32[512]{0:T(512)S(1)} %bitcast.512), channel_id=1, source_target_pairs={{0,128},{2,130},{4,132},{6,134},{8,136},{10,138},{12,140},{14,142}... | collective-permute-start | bytes 6152 | tf_op jit(solution)/shard_map/ppermute | solution.py:12
  840.9 41.9 %collective-permute-start.13 = (f32[512,256]{1,0:T(8,128)S(1)}, f32[512,256]{1,0:T(8,128)S(1)}, u32[]{:S(2)}, u32[]{:S(2)}) collective-permute-start(f32[512,256]{1,0:T(8,128)S(1)} %add.155), channel_id=1, source_target_pairs={{0,256},{2,258},{4,260},{6,262},{8,264},{10,266},{12,268},{14,270}... | collective-permute-start | bytes 1572872 | tf_op jit(solution)/shard_map/ppermute | solution.py:12
  865.4 16.9 %collective-permute-start.15 = (f32[512]{0:T(512)S(1)}, f32[512]{0:T(512)S(1)}, u32[]{:S(2)}, u32[]{:S(2)}) collective-permute-start(f32[512]{0:T(512)S(1)} %add.158), channel_id=1, source_target_pairs={{0,256},{2,258},{4,260},{6,262},{8,264},{10,266},{12,268},{14,270}... | collective-permute-start | bytes 6152 | tf_op jit(solution)/shard_map/ppermute | solution.py:12
  890.7 1.0 copy-start.21
  1049.3 1.0 copy-start.54
  1049.3 1.0 copy-start.8
  1049.3 1.0 copy-start.16
  1049.3 1.1 copy-start.29
  1049.3 1.2 copy-start.42
  1051.5 1.7 copy-start.52
  1052.2 1.0 copy-start.6
  1052.2 1.0 copy-start.14
  1052.2 1.1 copy-start.27
  1052.2 1.2 copy-start.40
  1054.3 1.7 copy-start.50
  1055.0 1.0 copy-start.4
  1055.0 1.0 copy-start.12
  1055.0 1.1 copy-start.25
  1055.0 1.2 copy-start.38
  1057.8 1.0 copy-start.10
  1057.8 1.0 copy-start.23
  1057.9 1.1 copy-start.36
  1063.6 4.7 copy-start.34
  1073.5 4.7 copy-start.33
  1083.4 4.9 copy-start.32
  1093.4 4.7 copy-start.31
  1102.0 2.7 copy-start.1
  (17 other events, 12.2 us)
where the time goes:
time: 1130 us; the launch traced here: 1100 us
  other arithmetic  635 us (56%)
  matrix products  142 us (13%)
  waiting for transfers between devices  105 us (9%)
  local copies, waits for them, and re-layouts  85.1 us (8%)
  starting transfers between devices  79.8 us (7%)
  blocking collectives  40.8 us (4%)
  between operations  16.2 us (1%)
    another operation x74, other arithmetic, invert_factor(): factor = jnp.linalg.cholesky(matrix_full)  418 us
    another operation x15, other arithmetic, invert_factor(): return jax.scipy.linalg.solve_triangular(factor, identity, lower=True)  204 us
    ppermute x16, waiting for transfers between devices, from_partner(): return lax.ppermute(value, axis, pairs)  104 us
    dot_general x60, matrix products, product(): jnp.dot(left, right, precision=highest, preferred_element_type=jnp.float32)  69.8 us
    ppermute x16, starting transfers between devices, from_partner(): return lax.ppermute(value, axis, pairs)  69.4 us
    another operation x66, local copies, waits for them, and re-layouts, invert_factor(): return jax.scipy.linalg.solve_triangular(factor, identity, lower=True)  57.5 us
    all_to_all x8, blocking collectives, copy_for_each(): return lax.all_to_all(copies, axis, split_axis=0, concat_axis=0, tiled=True)  40.8 us
    another operation x30, matrix products, invert_factor(): factor = jnp.linalg.cholesky(matrix_full)  34.3 us
  transfers between devices with their start and end apart: 17, of which 9 were waited for; matrix products, arithmetic and copies ran while one was open for 2% of the time, Pallas kernels for 0%

commit v1 on v0

v1 whole, which is shorter than its diff:
```python
import functools

import jax
import jax.numpy as jnp
from jax import lax
from jax.experimental import pallas as pl
from jax.experimental.pallas import tpu as pltpu
from jax.sharding import PartitionSpec as P

F32, BF16 = jnp.float32, jnp.bfloat16
MESH = pl.DeviceIdType.MESH
N = 512
HALF = N // 2
VMEM_SPEC = pl.BlockSpec(memory_space=pltpu.VMEM)
ANY_SPEC = pl.BlockSpec(memory_space=pl.ANY)
SMEM_SPEC = pl.BlockSpec(memory_space=pltpu.SMEM)
LIMIT = 60 * 1024 * 1024
NN = ((1,), (0,))
NT = ((1,), (1,))


def dot(a, b, dims=NN, precision=None):
    return lax.dot_general(a, b, (dims, ((), ())), precision=precision, preferred_element_type=F32)


def split(x):
    high = x.astype(BF16)
    return high, (x - high.astype(F32)).astype(BF16)


def split3(x):
    high = x.astype(BF16)
    rest = x - high.astype(F32)
    middle = rest.astype(BF16)
    return high, middle, (rest - middle.astype(F32)).astype(BF16)


def mm3(a, b, dims=NN):
    return dot(a[0], b[0], dims) + (dot(a[0], b[1], dims) + dot(a[1], b[0], dims))


def mm6(a, b):
    small = dot(a[0], b[2]) + (dot(a[1], b[1]) + dot(a[2], b[0]))
    return dot(a[0], b[0]) + ((dot(a[0], b[1]) + dot(a[1], b[0])) + small)


def eye(rows=N, cols=N, offset=0):
    return (
        lax.broadcasted_iota(jnp.int32, (rows, cols), 0) + offset == lax.broadcasted_iota(jnp.int32, (rows, cols), 1)
    ).astype(F32)


def invert(m_ref, out_ref, xb, rb, mh, mm, ml, alpha, low, steps):
    m = m_ref[...]
    mh[...], mm[...], ml[...] = split3(m)
    grown = 4.0 / ((1.0 + low) * (1.0 + low))
    xb[...] = ((grown * alpha) * ((1.0 + low) * eye() - alpha * m)).astype(BF16)

    def step(index, low):
        factor = 4.0 / ((1.0 + low) * (1.0 + low))
        rb[...] = ((1.0 + low) * eye() - dot(mh[...], xb[...])).astype(BF16)
        later = factor * low
        scale = jnp.where(index == steps - 1, factor * (2.0 / (1.0 + later)), factor)
        xb[...] = (scale * dot(xb[...], rb[...])).astype(BF16)
        return later

    lax.fori_loop(0, steps, step, jnp.float32(grown * low))
    resid = (eye() - dot(mh[...], xb[...])) - (dot(mm[...], xb[...]) + dot(ml[...], xb[...]))
    size = jnp.sum(resid * resid)
    rb[...] = resid.astype(BF16)
    square = dot(rb[...], rb[...])
    square_size = jnp.sum(square * square)
    rb[...], mh[...] = split(resid + square)
    out_ref[...] = xb[...].astype(F32) + (dot(xb[...], rb[...]) + dot(xb[...], mh[...]))

    @pl.when(jnp.logical_not(square_size < 4e-7))
    def _():
        rows = 64
        highest = lax.Precision.HIGHEST

        def run(resid_ref):
            out_ref[...] = jnp.where(size < 0.8, xb[...].astype(F32), alpha * eye())

            def more(state):
                return jnp.logical_and(state[0] < 80, jnp.logical_not(state[1] < 1e-7))

            def again(state):
                def measure(i, total):
                    at = pl.ds(pl.multiple_of(i * rows, rows), rows)
                    part = eye(rows, N, i * rows) - dot(m_ref[at, :], out_ref[...], precision=highest)
                    resid_ref[at, :] = part
                    return total + jnp.sum(part * part)

                total = lax.fori_loop(0, N // rows, measure, jnp.float32(0.0))

                def update(i, carry):
                    at = pl.ds(pl.multiple_of(i * rows, rows), rows)
                    out_ref[at, :] = out_ref[at, :] + dot(out_ref[at, :], resid_ref[...], precision=highest)
                    return carry

                lax.fori_loop(0, N // rows, update, 0)
                return state[0] + 1, total

            lax.while_loop(more, again, (jnp.int32(0), jnp.float32(1e30)))

        pl.run_scoped(run, pltpu.VMEM((N, N), F32))


INVERT_SCRATCH = [pltpu.VMEM((N, N), BF16)] * 5


def call(kernel, out_shape, ins, scratch, **params):
    return pl.pallas_call(
        kernel,
        out_shape=out_shape,
        in_specs=ins,
        out_specs=jax.tree.map(lambda _: VMEM_SPEC, out_shape),
        scratch_shapes=scratch,
        compiler_params=pltpu.CompilerParams(vmem_limit_bytes=LIMIT, **params),
    )


def leaf_kernel(live_ref, rows_ref, values_ref, pattern_ref, q_ref, v_ref, w_ref, m_ref, *scratch):
    blocks, wide = pattern_ref.shape
    width = N // wide
    row_of = lax.broadcasted_iota(jnp.int32, (wide, N), 0)
    spread = (lax.broadcasted_iota(jnp.int32, (wide, N), 1) // width == row_of).astype(F32)
    keep = dot(pattern_ref[...].astype(F32), spread)
    keep = jnp.where(lax.broadcasted_iota(jnp.int32, (blocks, N), 0) < live_ref[0], keep, 0.0)
    size = N // blocks
    masked = jnp.concatenate(
        [rows_ref[i * size : (i + 1) * size, :] * keep[i : i + 1, :].astype(BF16) for i in range(blocks)], axis=0
    )
    m = dot(masked, masked, ((0,), (0,))) + q_ref[...]
    m_ref[...] = m
    vector = mm3_row(values_ref[...], masked)
    bound = jnp.max(jnp.sum(jnp.abs(m), axis=0, keepdims=True)) * 1.00001
    invert(m_ref, v_ref, *scratch, 1.0 / bound, 1.0 / 64.0, 4)
    w_ref[...] = mm3(split(vector), split(v_ref[...]))


def mm3_row(values, right):
    high, rest = split(values)
    low = (values - high.astype(F32) - rest.astype(F32)).astype(BF16)
    return dot(high, right) + (dot(rest, right) + dot(low, right))


def tier_body(first, s_ref, u_ref, q_ref, g_ref, w_ref, m_ref, scratch):
    if first:
        m_ref[...] = 5.0 * eye() - mm6(split3(s_ref[...]), split3(q_ref[...]))
    else:
        m_ref[...] = 5.0 * eye() - s_ref[...]
    invert(m_ref, g_ref, *scratch, 1.0 / 5.001, 0.1999, 2)
    w_ref[...] = mm3(split(u_ref[...]), split(g_ref[...]), NT)


def tier1_kernel(s_ref, u_ref, q_ref, v_ref, g_ref, w_ref, r_ref, m_ref, *scratch):
    tier_body(True, s_ref, u_ref, q_ref, g_ref, w_ref, m_ref, scratch)
    half = pl.ds(pl.multiple_of(lax.axis_index("blk") * HALF, HALF), HALF)
    r_ref[...] = mm3(split(g_ref[...]), split(v_ref[:, half]))


def tier_kernel(s_ref, u_ref, r_in_ref, g_ref, w_ref, r_ref, m_ref, *scratch):
    tier_body(False, s_ref, u_ref, None, g_ref, w_ref, m_ref, scratch)
    r_ref[...] = mm3(split(g_ref[...]), split(r_in_ref[...]))


def root_kernel(
    s_ref, u_ref, r4_ref, r3_ref, r2_ref, g3_ref, g2_ref, g1_ref, v_ref, q_ref, w3_ref, w2_ref, w1_ref, w0_ref,
    mean_ref, cov_ref, g_ref, w_ref, m_ref, *scratch,
):
    tier_body(False, s_ref, u_ref, None, g_ref, w_ref, m_ref, scratch)
    q = mm3(split(g_ref[...]), split(r4_ref[...]))
    mean = w_ref[...]
    for r_ref, w_n_ref, g_n_ref in ((r4_ref, w3_ref, g3_ref), (r3_ref, w2_ref, g2_ref), (r2_ref, w1_ref, g1_ref)):
        gain = split(g_n_ref[...])
        q = r_ref[...] + mm3(gain, split(q))
        mean = w_n_ref[...] + mm3(split(mean), gain, NT)
    v = split(v_ref[...])
    info = split(q_ref[...])
    half = pl.ds(pl.multiple_of(lax.axis_index("blk") * HALF, HALF), HALF)
    cov_ref[...] = v_ref[:, half] + mm3(v, split(mm3(info, split(q))))
    mean = w0_ref[...] + mm3(split(mm3(split(mean), info)), v)
    mean_ref[...] = mean[0:1, :]


def place(leaf):
    return leaf // 16, (leaf // 4) % 4, leaf % 4


def comm_kernel(tier, g_ref, w_ref, s_ref, u_ref, parts, vecs, full, sems, send_sems, local_sem):
    leaf, core = lax.axis_index("leaf"), lax.axis_index("blk")
    z, y, x = place(leaf)
    if tier == 0:
        mine, stride = x, 1
    elif tier == 1:
        mine, stride = y, 4
    elif tier == 2:
        mine, stride = z % 4, 16
    else:
        mine, stride = z // 4, 64
    base = leaf - mine * stride

    def sibling(k):
        return base + ((mine + k) % 4) * stride

    def along_y(k):
        return leaf - y * 4 + ((y + k) % 4) * 4

    def along_x(k):
        return leaf - x + (x + k) % 4

    gather_y = tier >= 2
    peers = [sibling(k) for k in (1, 2, 3)]
    if gather_y:
        peers += [along_y(k) for k in (1, 2, 3)]
    if tier >= 1:
        peers += [along_x(k) for k in (1, 2, 3)]
    barrier = pltpu.get_barrier_semaphore()
    for peer in peers:
        pl.semaphore_signal(barrier, inc=1, device_id=(peer, core), device_id_type=MESH)
    pl.semaphore_signal(barrier, inc=1, device_id=(leaf, 1 - core), device_id_type=MESH)
    pl.semaphore_wait(barrier, len(peers) + 1)

    count = 16 if gather_y else 64
    quarter = N // 8

    def rows(c, x_at, y_at=None):
        start = c * HALF + x_at * quarter
        if y_at is not None:
            return pl.ds(pl.multiple_of(start + y_at * 16, 16), 16)
        return pl.ds(pl.multiple_of(start, quarter), quarter)

    def remote(src, dst, index, device):
        return pltpu.make_async_remote_copy(
            src_ref=src, dst_ref=dst, send_sem=send_sems.at[index], recv_sem=sems.at[index],
            device_id=device, device_id_type=MESH,
        )

    if tier == 0:
        own = rows(core, x)
    elif gather_y:
        own = rows(core, x, y)
    else:
        own = rows(core, x)
    first = []
    for k in (1, 2, 3):
        source = rows(core, (x + k) % 4) if tier == 0 else own
        first.append(remote(g_ref.at[source, :], parts.at[mine], k - 1, (sibling(k), core)))
        first.append(remote(w_ref, vecs.at[mine], 2 + k, (sibling(k), core)))
    for copy in first:
        copy.start()
    keep = pltpu.make_async_copy(g_ref.at[own, :], parts.at[mine], local_sem.at[0])
    keep_vec = pltpu.make_async_copy(w_ref, vecs.at[mine], local_sem.at[1])
    keep.start()
    keep_vec.start()
    keep.wait()
    keep_vec.wait()
    for copy in first:
        copy.wait()
    full[own, :] = (parts[0] + parts[1]) + (parts[2] + parts[3])
    u_ref[...] = (vecs[0] + vecs[1]) + (vecs[2] + vecs[3])
    if gather_y:
        second = [remote(full.at[own, :], full.at[own, :], 5 + k, (along_y(k), core)) for k in (1, 2, 3)]
        for copy in second:
            copy.start()
        for copy in second:
            copy.wait()
    quarter_rows = rows(core, x)
    third = [remote(full.at[quarter_rows, :], full.at[quarter_rows, :], 8 + k, (along_x(k), core)) for k in (1, 2, 3)]
    for copy in third:
        copy.start()
    partner = (leaf, 1 - core)
    last = [remote(full.at[quarter_rows, :], full.at[quarter_rows, :], 12, partner)]
    last[0].start()
    for k in (1, 2, 3):
        third[k - 1].wait_recv()
        arrived = rows(core, (x + 4 - k) % 4)
        copy = remote(full.at[arrived, :], full.at[arrived, :], 12 + k, partner)
        copy.start()
        last.append(copy)
    for copy in third:
        copy.wait_send()
    for copy in last:
        copy.wait()
    s_ref[...] = full[...]


def comm(tier, g, w):
    count = 16 if tier >= 2 else 64
    return pl.pallas_call(
        functools.partial(comm_kernel, tier),
        out_shape=(jax.ShapeDtypeStruct((N, N), F32), jax.ShapeDtypeStruct((8, N), F32)),
        in_specs=[VMEM_SPEC, VMEM_SPEC],
        out_specs=(VMEM_SPEC, VMEM_SPEC),
        scratch_shapes=[
            pltpu.VMEM((4, count, N), F32),
            pltpu.VMEM((4, 8, N), F32),
            pltpu.VMEM((N, N), F32),
            pltpu.SemaphoreType.DMA((16,)),
            pltpu.SemaphoreType.DMA((16,)),
            pltpu.SemaphoreType.DMA((2,)),
        ],
        compiler_params=pltpu.CompilerParams(vmem_limit_bytes=LIMIT, collective_id=tier, has_side_effects=True),
    )(g, w)


def matrix(rows=N, cols=N, dtype=F32):
    return jax.ShapeDtypeStruct((rows, cols), dtype)


def leaf_call(obs_rows, obs_values, track_blocks, pattern, process_info):
    values = jnp.broadcast_to(obs_values[None, :], (8, N))
    return call(
        leaf_kernel, (matrix(), matrix(8)), [SMEM_SPEC] + [VMEM_SPEC] * 4, [pltpu.VMEM((N, N), F32)] + INVERT_SCRATCH
    )(track_blocks, obs_rows, values, pattern, process_info)


def tier1_call(s, u, q, v):
    return call(
        tier1_kernel, (matrix(), matrix(8), matrix(N, HALF)), [VMEM_SPEC] * 4, [pltpu.VMEM((N, N), F32)] + INVERT_SCRATCH
    )(s, u, q, v)


def tier_call(s, u, r):
    return call(
        tier_kernel, (matrix(), matrix(8), matrix(N, HALF)), [VMEM_SPEC] * 3, [pltpu.VMEM((N, N), F32)] + INVERT_SCRATCH
    )(s, u, r)


def root_call(*args):
    return call(
        root_kernel,
        (matrix(1), matrix(N, HALF)),
        [VMEM_SPEC] * 14,
        [pltpu.VMEM((N, N), F32), pltpu.VMEM((8, N), F32), pltpu.VMEM((N, N), F32)] + INVERT_SCRATCH,
    )(*args)


def shards(obs_rows, obs_values, track_blocks, pattern, process_info):
    v0, w0 = leaf_call(obs_rows, obs_values, track_blocks, pattern, process_info)
    s, u = comm(0, v0, w0)
    g1, w1, r2 = tier1_call(s, u, process_info, v0)
    s, u = comm(1, g1, w1)
    g2, w2, r3 = tier_call(s, u, r2)
    s, u = comm(2, g2, w2)
    g3, w3, r4 = tier_call(s, u, r3)
    s, u = comm(3, g3, w3)
    return root_call(s, u, r4, r3, r2, g3, g2, g1, v0, process_info, w3, w2, w1, w0)


def solution(mesh):
    placed = (P("leaf", None), P("leaf"), P("leaf"), P("leaf", None), P())
    return jax.shard_map(
        shards,
        mesh=mesh,
        in_specs=placed,
        out_specs=(P("leaf", None), P("leaf", "blk")),
        check_vma=False,
    )
```

time: 1130 us -> 163 us (0.14); the launches traced: 1100 us -> 161 us
  other arithmetic: 635 us -> 0 us
  Pallas kernels: 0 us -> 158 us
  matrix products: 142 us -> 0 us
  waiting for transfers between devices: 105 us -> 0 us
  local copies, waits for them, and re-layouts: 85.1 us -> 1.29 us
  starting transfers between devices: 79.8 us -> 0 us
  blocking collectives: 40.8 us -> 0 us
  between operations: 16.2 us -> 1.31 us
    another operation x89 -> x0, other arithmetic: 622 us -> none  [the longest x74 418 us: invert_factor(): factor = jnp.linalg.cholesky(matrix_full)]
    pallas_call x0 -> x9, Pallas kernels: none -> 158 us  [the longest x4 110 us: comm(): pl.pallas_call(functools.partial(comm_kernel, tier), out_shape=(jax.Shape...]
    ppermute x16 -> x0, waiting for transfers between devices: 104 us -> none  [from_partner(): return lax.ppermute(value, axis, pairs)]
    dot_general x66 -> x0, matrix products: 77.9 us -> none  [the longest x60 69.8 us: product(): jnp.dot(left, right, precision=highest, preferred_element_type=jnp.float32)]
    ppermute x16 -> x0, starting transfers between devices: 69.4 us -> none  [from_partner(): return lax.ppermute(value, axis, pairs)]
    another operation x65 -> x0, matrix products: 64.1 us -> none  [the longest x30 34.3 us: invert_factor(): factor = jnp.linalg.cholesky(matrix_full)]
    another operation x86 -> x0, local copies, waits for them, and re-layouts: 60.7 us -> none  [the longest x66 57.5 us: invert_factor(): return jax.scipy.linalg.solve_triangular(factor, identity, lower=True)]
    all_to_all x8 -> x0, blocking collectives: 40.8 us -> none  [copy_for_each(): return lax.all_to_all(copies, axis, split_axis=0, concat_axis=0, tiled=True)]
  transfers between devices with their start and end apart: 17 -> 0, of which waited for: 9 -> 0; matrix products, arithmetic and copies ran while one was open for 2% -> 0% of each run, Pallas kernels for 0% -> 0%
where the time goes in v1:
time: 163 us; the launch traced here: 161 us
  Pallas kernels  158 us (97%)
    pallas_call x4, Pallas kernels, comm(): pl.pallas_call(functools.partial(comm_kernel, tier), out_shape=(jax.Shape...  110 us
    pallas_call x2, Pallas kernels, tier_call(): call(tier_kernel, (matrix(), matrix(8), matrix(N, HALF)), [VMEM_SPEC] * 3...  15.5 us
    pallas_call x1, Pallas kernels, root_call(): call(root_kernel, (matrix(1), matrix(N, HALF)), [VMEM_SPEC] * 14, [pltpu....  14.6 us
    pallas_call x1, Pallas kernels, tier1_call(): call(tier1_kernel, (matrix(), matrix(8), matrix(N, HALF)), [VMEM_SPEC] *...  9.62 us
    pallas_call x1, Pallas kernels, leaf_call(): call(leaf_kernel, (matrix(), matrix(8)), [SMEM_SPEC] + [VMEM_SPEC] * 4, [...  8.86 us

profile of v1, /device:TPU:1, one launch (start us, length us, event | category | flops | bytes accessed | tf_op | source)
XLA Modules:
  0.0 160.7 jit_solution(8801754587009243362)
XLA Ops:
  1.3 1.3 broadcast_in_dim.2.values_ref
  2.6 8.9 %shard_map.68 = (f32[512,512]{1,0:T(8,128)}, f32[8,512]{1,0:T(8,128)}) custom-call(s32[1]{0:T(128)S(6)} %copy.7.live_ref, bf16[512,512]{1,0:T(8,128)(2,1)} %rows_ref.1, f32[8,512]{1,0:T(8,128)} %broadcast_in_dim.2.values_ref, s32[4,64]{1,0:T(4,128)} %pattern_ref.1, f32[512,512]{1,0:T(8,128)} %q_ref.5), custom_call_target="tpu_custom_call" | custom-call | tf_op jit(solution)/shard_map/pallas_call | solution.py:314
  11.4 28.8 %shard_map.69 = (f32[512,512]{1,0:T(8,128)}, f32[8,512]{1,0:T(8,128)}) custom-call(f32[512,512]{1,0:T(8,128)} %get-tuple-element.21.g_ref.v_ref, f32[8,512]{1,0:T(8,128)} %get-tuple-element.22.w_ref.w0_ref), custom_call_target="tpu_custom_call" | custom-call | tf_op jit(solution)/shard_map/pallas_call | solution.py:291
  40.2 9.6 %shard_map.70 = (f32[512,512]{1,0:T(8,128)}, f32[8,512]{1,0:T(8,128)}, f32[512,256]{1,0:T(8,128)}) custom-call(f32[512,512]{1,0:T(8,128)} %get-tuple-element.23.s_ref, f32[8,512]{1,0:T(8,128)} %get-tuple-element.24.u_ref, f32[512,512]{1,0:T(8,128)} %q_ref.5, f32[512,512]{1,0:T(8,128)} %get-tuple-element.21.g_ref.v_ref), custom_call_target="tpu_custom_call" | custom-call | tf_op jit(solution)/shard_map/pallas_call | solution.py:320
  49.8 21.1 %shard_map.71 = (f32[512,512]{1,0:T(8,128)}, f32[8,512]{1,0:T(8,128)}) custom-call(f32[512,512]{1,0:T(8,128)} %get-tuple-element.25.g_ref.g1_ref, f32[8,512]{1,0:T(8,128)} %get-tuple-element.26.w_ref.w1_ref), custom_call_target="tpu_custom_call" | custom-call | tf_op jit(solution)/shard_map/pallas_call | solution.py:291
  71.0 7.6 %shard_map.72 = (f32[512,512]{1,0:T(8,128)}, f32[8,512]{1,0:T(8,128)}, f32[512,256]{1,0:T(8,128)}) custom-call(f32[512,512]{1,0:T(8,128)} %get-tuple-element.27.s_ref, f32[8,512]{1,0:T(8,128)} %get-tuple-element.28.u_ref, f32[512,256]{1,0:T(8,128)} %get-tuple-element.29.r_in_ref.r2_ref), custom_call_target="tpu_custom_call" | custom-call | tf_op jit(solution)/shard_map/pallas_call | solution.py:326
  78.6 24.9 %shard_map.73 = (f32[512,512]{1,0:T(8,128)}, f32[8,512]{1,0:T(8,128)}) custom-call(f32[512,512]{1,0:T(8,128)} %get-tuple-element.30.g_ref.g2_ref, f32[8,512]{1,0:T(8,128)} %get-tuple-element.31.w_ref.w2_ref), custom_call_target="tpu_custom_call" | custom-call | tf_op jit(solution)/shard_map/pallas_call | solution.py:291
  103.5 7.9 %shard_map.74 = (f32[512,512]{1,0:T(8,128)}, f32[8,512]{1,0:T(8,128)}, f32[512,256]{1,0:T(8,128)}) custom-call(f32[512,512]{1,0:T(8,128)} %get-tuple-element.32.s_ref, f32[8,512]{1,0:T(8,128)} %get-tuple-element.33.u_ref, f32[512,256]{1,0:T(8,128)} %get-tuple-element.34.r_in_ref.r3_ref), custom_call_target="tpu_custom_call" | custom-call | tf_op jit(solution)/shard_map/pallas_call | solution.py:326
  111.4 34.7 %shard_map.75 = (f32[512,512]{1,0:T(8,128)}, f32[8,512]{1,0:T(8,128)}) custom-call(f32[512,512]{1,0:T(8,128)} %get-tuple-element.35.g_ref.g3_ref, f32[8,512]{1,0:T(8,128)} %get-tuple-element.36.w_ref.w3_ref), custom_call_target="tpu_custom_call" | custom-call | tf_op jit(solution)/shard_map/pallas_call | solution.py:291
  146.2 14.6 %shard_map.76 = (f32[1,512]{1,0:T(1,128)}, f32[512,256]{1,0:T(8,128)}) custom-call(f32[512,512]{1,0:T(8,128)} %get-tuple-element.37.s_ref, f32[8,512]{1,0:T(8,128)} %get-tuple-element.38.u_ref, f32[512,256]{1,0:T(8,128)} %get-tuple-element.39.r4_ref, f32[512,256]{1,0:T(8,128)} %get-tuple-element.34.r_in_ref.r3_ref, ...), custom_call_target="tpu_custom_call" | custom-call | tf_op jit(solution)/shard_map/pallas_call | solution.py:332

commit v2 on v1

v2 whole, which is shorter than its diff:
```python
import functools

import jax
import jax.numpy as jnp
from jax import lax
from jax.experimental import pallas as pl
from jax.experimental.pallas import tpu as pltpu
from jax.sharding import PartitionSpec as P

F32, BF16 = jnp.float32, jnp.bfloat16
MESH = pl.DeviceIdType.MESH
N = 512
HALF = N // 2
VMEM_SPEC = pl.BlockSpec(memory_space=pltpu.VMEM)
ANY_SPEC = pl.BlockSpec(memory_space=pl.ANY)
SMEM_SPEC = pl.BlockSpec(memory_space=pltpu.SMEM)
LIMIT = 60 * 1024 * 1024
NN = ((1,), (0,))
NT = ((1,), (1,))


def dot(a, b, dims=NN, precision=None):
    return lax.dot_general(a, b, (dims, ((), ())), precision=precision, preferred_element_type=F32)


def split(x):
    high = x.astype(BF16)
    return high, (x - high.astype(F32)).astype(BF16)


def split3(x):
    high = x.astype(BF16)
    rest = x - high.astype(F32)
    middle = rest.astype(BF16)
    return high, middle, (rest - middle.astype(F32)).astype(BF16)


def mm3(a, b, dims=NN):
    return dot(a[0], b[0], dims) + (dot(a[0], b[1], dims) + dot(a[1], b[0], dims))


def mm6(a, b):
    small = dot(a[0], b[2]) + (dot(a[1], b[1]) + dot(a[2], b[0]))
    return dot(a[0], b[0]) + ((dot(a[0], b[1]) + dot(a[1], b[0])) + small)


def eye(rows=N, cols=N, offset=0):
    return (
        lax.broadcasted_iota(jnp.int32, (rows, cols), 0) + offset == lax.broadcasted_iota(jnp.int32, (rows, cols), 1)
    ).astype(F32)


def invert(m_ref, xb, rb, mh, mm, ml, alpha, low, steps):
    m = m_ref[...]
    mh[...], mm[...], ml[...] = split3(m)
    grown = 4.0 / ((1.0 + low) * (1.0 + low))
    xb[...] = ((grown * alpha) * ((1.0 + low) * eye() - alpha * m)).astype(BF16)

    def step(index, low):
        factor = 4.0 / ((1.0 + low) * (1.0 + low))
        rb[...] = ((1.0 + low) * eye() - dot(mh[...], xb[...])).astype(BF16)
        later = factor * low
        scale = jnp.where(index == steps - 1, factor * (2.0 / (1.0 + later)), factor)
        xb[...] = (scale * dot(xb[...], rb[...])).astype(BF16)
        return later

    lax.fori_loop(0, steps, step, jnp.float32(grown * low))
    resid = (eye() - dot(mh[...], xb[...])) - (dot(mm[...], xb[...]) + dot(ml[...], xb[...]))
    rb[...] = resid.astype(BF16)
    square = dot(rb[...], rb[...])
    rb[...], mh[...] = split(resid + square)
    return jnp.sum(square * square, keepdims=True)


def finish(out_ref, xb, rb, mh):
    out_ref[...] = xb[...].astype(F32) + (dot(xb[...], rb[...]) + dot(xb[...], mh[...]))


def mm3_row(values, right):
    high, rest, low = split3(values)
    return dot(high, right) + (dot(rest, right) + dot(low, right))


def flagged(vector, below, missed):
    row = lax.broadcasted_iota(jnp.int32, (8, N), 0)
    return jnp.where(row == 1, below + jnp.where(missed < 4e-7, 0.0, 1.0), jnp.where(row == 0, vector, 0.0))


def place(leaf):
    return leaf // 16, (leaf // 4) % 4, leaf % 4


def group(tier, leaf):
    z, y, x = place(leaf)
    return ((x, 1), (y, 4), (z % 4, 16), (z // 4, 64))[tier]


def ring(leaf, mine, stride, k):
    return leaf - mine * stride + ((mine + k) % 4) * stride


PARTNER = 21
SEMS = PARTNER + 8


def exchange(tier, g_ref, w_ref, parts, vecs, full, u_ref, send_sems, recv_sems, sent, meanwhile):
    leaf, core = lax.axis_index("leaf"), lax.axis_index("blk")
    z, y, x = place(leaf)
    mine, stride = group(tier, leaf)
    gather_y = tier >= 2
    eighth = N // 8

    def quarter(c, x_at):
        return pl.ds(pl.multiple_of(c * HALF + x_at * eighth, eighth), eighth)

    def cols(h):
        return pl.ds(h * HALF, HALF)

    def remote(src, dst, index, device):
        copy = pltpu.make_async_remote_copy(
            src_ref=src, dst_ref=dst, send_sem=send_sems.at[tier, index], recv_sem=recv_sems.at[tier, index],
            device_id=device, device_id_type=MESH,
        )
        copy.start()
        sent.append(copy)
        return copy

    def spread(rows, h, start, mine, stride):
        part = full.at[tier, rows, cols(h)]
        return [remote(part, part, start + 3 * h + k - 1, (ring(leaf, mine, stride, k), core)) for k in (1, 2, 3)]

    own = quarter(core, x)
    if gather_y:
        own = pl.ds(pl.multiple_of(core * HALF + x * eighth + y * 16, 16), 16)
    first = [[], []]
    for h in (0, 1):
        for k in (1, 2, 3):
            source = quarter(core, (x + k) % 4) if tier == 0 else own
            first[h].append(
                remote(
                    g_ref.at[source, cols(h)], parts.at[mine, :, cols(h)], 3 * h + k - 1,
                    (ring(leaf, mine, stride, k), core),
                )
            )
        if h == 0:
            vectors = [
                remote(w_ref, vecs.at[tier, mine], 5 + k, (ring(leaf, mine, stride, k), core)) for k in (1, 2, 3)
            ]
    parts[mine, :, :] = g_ref[own, :]
    vecs[tier, mine] = w_ref[...]
    meanwhile()
    along_y, along_x, halves = [], [], []

    def to_x(h):
        along_x.append(spread(quarter(core, x), h, 15, x, 1))
        to_partner(h, 0)

    def to_partner(h, k):
        part = full.at[tier, quarter(core, (x + 4 - k) % 4), cols(h)]
        halves.append(remote(part, part, PARTNER + 4 * h + k, (leaf, 1 - core)))

    for h in (0, 1):
        for copy in first[h]:
            copy.wait_recv()
        at = slice(h * HALF, (h + 1) * HALF)
        full[tier, own, at] = (parts[0, :, at] + parts[1, :, at]) + (parts[2, :, at] + parts[3, :, at])
        if gather_y:
            along_y.append(spread(own, h, 9, y, 4))
        else:
            to_x(h)
    for h in (0, 1):
        if gather_y:
            for copy in along_y[h]:
                copy.wait_recv()
            to_x(h)
    for copy in vectors:
        copy.wait_recv()
    u_ref[...] = (vecs[tier, 0] + vecs[tier, 1]) + (vecs[tier, 2] + vecs[tier, 3])
    for h in (0, 1):
        for k in (1, 3, 2):
            along_x[h][k - 1].wait_recv()
            to_partner(h, k)
    for copy in halves:
        copy.wait_recv()


def smoother_kernel(
    live_ref, rows_ref, values_ref, pattern_ref, q_ref, mean_ref, cov_ref, missed_ref,
    g, m_ref, xb, rb, mh, mm, ml, gh, gl, vh, vl, qh, ql, r, w, u_ref, full, vecs, parts0, parts1, parts2, parts3,
    send_sems, recv_sems,
):
    leaf, core = lax.axis_index("leaf"), lax.axis_index("blk")
    barrier = pltpu.get_barrier_semaphore()
    for tier in range(4):
        mine, stride = group(tier, leaf)
        for k in (1, 2, 3):
            peer = (ring(leaf, mine, stride, k), core)
            pl.semaphore_signal(barrier, inc=1, device_id=peer, device_id_type=MESH)
    pl.semaphore_signal(barrier, inc=1, device_id=(leaf, 1 - core), device_id_type=MESH)

    blocks, wide = pattern_ref.shape
    row_of = lax.broadcasted_iota(jnp.int32, (wide, N), 0)
    widen = (lax.broadcasted_iota(jnp.int32, (wide, N), 1) // (N // wide) == row_of).astype(F32)
    keep = dot(pattern_ref[...].astype(F32), widen)
    keep = jnp.where(lax.broadcasted_iota(jnp.int32, (blocks, N), 0) < live_ref[0], keep, 0.0)
    size = N // blocks
    masked = jnp.concatenate(
        [rows_ref[i * size : (i + 1) * size, :] * keep[i : i + 1, :].astype(BF16) for i in range(blocks)], axis=0
    )
    m = dot(masked, masked, ((0,), (0,))) + q_ref[...]
    m_ref[...] = m
    vector = mm3_row(jnp.broadcast_to(values_ref[...], (8, N)), masked)
    bound = jnp.max(jnp.sum(jnp.abs(m), axis=0, keepdims=True)) * 1.00001
    missed = invert(m_ref, xb, rb, mh, mm, ml, 1.0 / bound, 1.0 / 64.0, 4)
    v_ref = g.at[0]
    finish(v_ref, xb, rb, mh)
    vh[...], vl[...] = split(v_ref[...])
    w[0] = flagged(mm3(split(vector), (vh[...], vl[...])), 0.0, missed)
    pl.semaphore_wait(barrier, 13)

    half = pl.ds(pl.multiple_of(core * HALF, HALF), HALF)
    parts = (parts0, parts1, parts2, parts3)
    sent = []

    def meanwhile_leaf():
        qh[...], ql[...] = split(q_ref[...])
        r[0] = v_ref[:, half]

    def meanwhile_tier(n):
        def work():
            r[n] = mm3((gh[n - 1], gl[n - 1]), split(r[n - 1]))

        return work

    for tier in range(4):
        exchange(
            tier, g.at[tier], w.at[tier], parts[tier], vecs, full, u_ref, send_sems, recv_sems, sent,
            meanwhile_leaf if tier == 0 else meanwhile_tier(tier),
        )
        if tier == 0:
            m_ref[...] = 5.0 * eye() - mm6(split3(full[0]), split3(q_ref[...]))
        else:
            m_ref[...] = 5.0 * eye() - full[tier]
        missed = invert(m_ref, xb, rb, mh, mm, ml, 1.0 / 5.001, 0.1999, 2)
        u = u_ref[...]
        if tier < 3:
            g_ref = g.at[tier + 1]
            finish(g_ref, xb, rb, mh)
            gh[tier], gl[tier] = split(g_ref[...])
            w[tier + 1] = flagged(mm3(split(u), (gh[tier], gl[tier]), NT), u, missed)
        else:
            u = u + mm3(split(u), (rb[...], mh[...]), NT)
            uh, ul = split(u)
            mean = dot(uh, xb[...], NT) + dot(ul, xb[...], NT)
            missed_ref[...] = (u_ref[1:2, 0:128] + jnp.where(missed < 4e-7, 0.0, 1.0)) * jnp.ones((8, 128), F32)
            q = r[3] + mm3((rb[...], mh[...]), split(r[3]))
            q_high, q_low = split(q)
            q = dot(xb[...], q_high) + dot(xb[...], q_low)
    for n in (3, 2, 1):
        gain = (gh[n - 1], gl[n - 1])
        q = r[n] + mm3(gain, split(q))
        mean = w[n] + mm3(split(mean), gain, NT)
    info = (qh[...], ql[...])
    v = (vh[...], vl[...])
    cov_ref[...] = r[0] + mm3(v, split(mm3(info, split(q))))
    mean = w[0] + mm3(split(mm3(split(mean), info)), v)
    mean_ref[...] = mean[0:1, :]
    for copy in sent:
        copy.wait_send()


def matrix(rows=N, cols=N, dtype=F32):
    return jax.ShapeDtypeStruct((rows, cols), dtype)


def smoother(obs_rows, obs_values, track_blocks, pattern, process_info):
    def square(count, dtype):
        return pltpu.VMEM((count, N, N) if count > 1 else (N, N), dtype)

    return pl.pallas_call(
        smoother_kernel,
        out_shape=(matrix(1), matrix(N, HALF), matrix(8, 128)),
        in_specs=[SMEM_SPEC] + [VMEM_SPEC] * 4,
        out_specs=(VMEM_SPEC,) * 3,
        scratch_shapes=[
            square(4, F32), square(1, F32), *[square(1, BF16)] * 5, square(3, BF16), square(3, BF16), *[square(1, BF16)] * 4,
            pltpu.VMEM((4, N, HALF), F32), pltpu.VMEM((4, 8, N), F32), pltpu.VMEM((8, N), F32), square(4, F32),
            pltpu.VMEM((4, 4, 8, N), F32),
            *[pltpu.VMEM((4, rows, N), F32) for rows in (64, 64, 16, 16)],
            pltpu.SemaphoreType.DMA((4, SEMS)), pltpu.SemaphoreType.DMA((4, SEMS)),
        ],
        compiler_params=pltpu.CompilerParams(vmem_limit_bytes=LIMIT, collective_id=0, has_side_effects=True),
    )(track_blocks, obs_rows, obs_values[None, :], pattern, process_info)


ROWS = 64
DEPTH = 128


def chunk(i, size):
    return pl.ds(pl.multiple_of(i * size, size), size)


def careful_rows(left_ref, right_ref, at):
    def add(j, total):
        piece = dot(left_ref[at, chunk(j, DEPTH)], right_ref[chunk(j, DEPTH), :], precision=lax.Precision.HIGHEST)
        return total + piece

    return lax.fori_loop(0, N // DEPTH, add, jnp.zeros((ROWS, right_ref.shape[1]), F32))


def careful_inverse_kernel(alpha_ref, m_ref, out_ref, resid_ref):
    out_ref[...] = alpha_ref[0] * eye()

    def more(state):
        return jnp.logical_and(state[0] < 80, jnp.logical_not(state[1] < 1e-7))

    def again(state):
        def measure(i, total):
            at = chunk(i, ROWS)
            part = eye(ROWS, N, i * ROWS) - careful_rows(m_ref, out_ref, at)
            resid_ref[at, :] = part
            return total + jnp.sum(part * part)

        total = lax.fori_loop(0, N // ROWS, measure, jnp.float32(0.0))

        def update(i, carry):
            at = chunk(i, ROWS)
            out_ref[at, :] = out_ref[at, :] + careful_rows(out_ref, resid_ref, at)
            return carry

        lax.fori_loop(0, N // ROWS, update, 0)
        return state[0] + 1, total

    lax.while_loop(more, again, (jnp.int32(0), jnp.float32(1e30)))


def careful_inverse(m, alpha):
    return pl.pallas_call(
        careful_inverse_kernel,
        out_shape=matrix(),
        in_specs=[SMEM_SPEC, VMEM_SPEC],
        out_specs=VMEM_SPEC,
        scratch_shapes=[pltpu.VMEM((N, N), F32)],
        compiler_params=pltpu.CompilerParams(vmem_limit_bytes=LIMIT),
    )(jnp.reshape(alpha, (1,)), m)


def careful_product_kernel(left_ref, right_ref, out_ref):
    def work(i, carry):
        at = chunk(i, ROWS)
        out_ref[at, :] = careful_rows(left_ref, right_ref, at)
        return carry

    lax.fori_loop(0, N // ROWS, work, 0)


def careful_product(left, right):
    return pl.pallas_call(
        careful_product_kernel,
        out_shape=matrix(N, right.shape[1]),
        in_specs=[VMEM_SPEC, VMEM_SPEC],
        out_specs=VMEM_SPEC,
        compiler_params=pltpu.CompilerParams(vmem_limit_bytes=LIMIT),
    )(left, right)


def comm_kernel(tier, g_ref, w_ref, s_ref, u_ref, parts, vecs, full, sems, send_sems, local_sem):
    leaf, core = lax.axis_index("leaf"), lax.axis_index("blk")
    z, y, x = place(leaf)
    if tier == 0:
        mine, stride = x, 1
    elif tier == 1:
        mine, stride = y, 4
    elif tier == 2:
        mine, stride = z % 4, 16
    else:
        mine, stride = z // 4, 64
    base = leaf - mine * stride

    def sibling(k):
        return base + ((mine + k) % 4) * stride

    def along_y(k):
        return leaf - y * 4 + ((y + k) % 4) * 4

    def along_x(k):
        return leaf - x + (x + k) % 4

    gather_y = tier >= 2
    peers = [sibling(k) for k in (1, 2, 3)]
    if gather_y:
        peers += [along_y(k) for k in (1, 2, 3)]
    if tier >= 1:
        peers += [along_x(k) for k in (1, 2, 3)]
    barrier = pltpu.get_barrier_semaphore()
    for peer in peers:
        pl.semaphore_signal(barrier, inc=1, device_id=(peer, core), device_id_type=MESH)
    pl.semaphore_signal(barrier, inc=1, device_id=(leaf, 1 - core), device_id_type=MESH)
    pl.semaphore_wait(barrier, len(peers) + 1)

    count = 16 if gather_y else 64
    quarter = N // 8

    def rows(c, x_at, y_at=None):
        start = c * HALF + x_at * quarter
        if y_at is not None:
            return pl.ds(pl.multiple_of(start + y_at * 16, 16), 16)
        return pl.ds(pl.multiple_of(start, quarter), quarter)

    def remote(src, dst, index, device):
        return pltpu.make_async_remote_copy(
            src_ref=src, dst_ref=dst, send_sem=send_sems.at[index], recv_sem=sems.at[index],
            device_id=device, device_id_type=MESH,
        )

    if tier == 0:
        own = rows(core, x)
    elif gather_y:
        own = rows(core, x, y)
    else:
        own = rows(core, x)
    first = []
    for k in (1, 2, 3):
        source = rows(core, (x + k) % 4) if tier == 0 else own
        first.append(remote(g_ref.at[source, :], parts.at[mine], k - 1, (sibling(k), core)))
        first.append(remote(w_ref, vecs.at[mine], 2 + k, (sibling(k), core)))
    for copy in first:
        copy.start()
    keep = pltpu.make_async_copy(g_ref.at[own, :], parts.at[mine], local_sem.at[0])
    keep_vec = pltpu.make_async_copy(w_ref, vecs.at[mine], local_sem.at[1])
    keep.start()
    keep_vec.start()
    keep.wait()
    keep_vec.wait()
    for copy in first:
        copy.wait()
    full[own, :] = (parts[0] + parts[1]) + (parts[2] + parts[3])
    u_ref[...] = (vecs[0] + vecs[1]) + (vecs[2] + vecs[3])
    if gather_y:
        second = [remote(full.at[own, :], full.at[own, :], 5 + k, (along_y(k), core)) for k in (1, 2, 3)]
        for copy in second:
            copy.start()
        for copy in second:
            copy.wait()
    quarter_rows = rows(core, x)
    third = [remote(full.at[quarter_rows, :], full.at[quarter_rows, :], 8 + k, (along_x(k), core)) for k in (1, 2, 3)]
    for copy in third:
        copy.start()
    partner = (leaf, 1 - core)
    last = [remote(full.at[quarter_rows, :], full.at[quarter_rows, :], 12, partner)]
    last[0].start()
    for k in (1, 2, 3):
        third[k - 1].wait_recv()
        arrived = rows(core, (x + 4 - k) % 4)
        copy = remote(full.at[arrived, :], full.at[arrived, :], 12 + k, partner)
        copy.start()
        last.append(copy)
    for copy in third:
        copy.wait_send()
    for copy in last:
        copy.wait()
    s_ref[...] = full[...]


def comm(tier, g, w):
    count = 16 if tier >= 2 else 64
    return pl.pallas_call(
        functools.partial(comm_kernel, tier),
        out_shape=(jax.ShapeDtypeStruct((N, N), F32), jax.ShapeDtypeStruct((8, N), F32)),
        in_specs=[VMEM_SPEC, VMEM_SPEC],
        out_specs=(VMEM_SPEC, VMEM_SPEC),
        scratch_shapes=[
            pltpu.VMEM((4, count, N), F32),
            pltpu.VMEM((4, 8, N), F32),
            pltpu.VMEM((N, N), F32),
            pltpu.SemaphoreType.DMA((16,)),
            pltpu.SemaphoreType.DMA((16,)),
            pltpu.SemaphoreType.DMA((2,)),
        ],
        compiler_params=pltpu.CompilerParams(vmem_limit_bytes=LIMIT, collective_id=tier + 1, has_side_effects=True),
    )(g, w)


def careful(obs_rows, obs_values, track_blocks, pattern, process_info):
    blocks, wide = pattern.shape
    keep = jnp.repeat(pattern.astype(BF16), N // wide, axis=1)
    keep = keep * (jnp.arange(blocks) < track_blocks[0]).astype(BF16)[:, None]
    masked = (obs_rows.reshape(blocks, -1, N) * keep[:, None, :]).reshape(-1, N)
    m = jnp.dot(masked.T, masked, preferred_element_type=F32) + process_info
    v = careful_inverse(m, 1.0 / (jnp.max(jnp.sum(jnp.abs(m), axis=0)) * 1.00001))

    def column(vector):
        return jnp.broadcast_to(vector[:, None], (N, 128))

    w0 = careful_product(v, careful_product(masked.T.astype(F32), column(obs_values)))
    g, w = v, w0
    r0 = lax.dynamic_slice_in_dim(v, lax.axis_index("blk") * HALF, HALF, 1)
    r, gains, kept = r0, [], []
    for tier in range(4):
        s, u = comm(tier, g, jnp.broadcast_to(w[:, 0][None, :], (8, N)))
        if tier == 0:
            s = careful_product(s, process_info)
        g = careful_inverse(5.0 * jnp.eye(N, dtype=F32) - s, jnp.float32(1.0 / 5.001))
        both = careful_product(g, jnp.concatenate([r, column(u[0])], axis=1))
        r, w = both[:, :HALF], both[:, HALF:]
        gains.append(g)
        kept.append(both)

    def down(state, of_tier):
        gain, own = of_tier
        return own + careful_product(gain, state), None

    state, _ = lax.scan(down, kept[3], (jnp.stack(gains[2::-1]), jnp.stack(kept[2::-1])))
    state = careful_product(v, careful_product(process_info, state))
    return (w0[:, 0] + state[:, HALF])[None, :], r0 + state[:, :HALF]


def shards(*args):
    mean, cov, missed = smoother(*args)
    return lax.cond(missed[0, 0] > 0.5, lambda: careful(*args), lambda: (mean, cov))


def solution(mesh):
    placed = (P("leaf", None), P("leaf"), P("leaf"), P("leaf", None), P())
    return jax.shard_map(
        shards,
        mesh=mesh,
        in_specs=placed,
        out_specs=(P("leaf", None), P("leaf", "blk")),
        check_vma=False,
    )
```

time: 163 us -> 126 us (0.77); the launches traced: 161 us -> 126 us
  Pallas kernels: 158 us -> 120 us
  local copies, waits for them, and re-layouts: 1.29 us -> 3.64 us
    pallas_call x9 -> x1, Pallas kernels: 158 us -> 120 us  [smoother(): pl.pallas_call(smoother_kernel, out_shape=(matrix(1), matrix(N, HALF), ma...]
    unnamed x0 -> x2, local copies, waits for them, and re-layouts: none -> 2.45 us
where the time goes in v2:
time: 126 us
  Pallas kernels  120 us (95%)
  local copies, waits for them, and re-layouts  3.64 us (3%)
  between operations  1.95 us (2%)
    pallas_call x1, Pallas kernels, smoother(): pl.pallas_call(smoother_kernel, out_shape=(matrix(1), matrix(N, HALF), ma...  120 us

profile of v2, /device:TPU:1, one launch (start us, length us, event | category | flops | bytes accessed | tf_op | source)
XLA Modules:
  0.0 125.8 jit_solution(3556772859319073177)
XLA Ops:
  1.3 120.2 %shard_map.72 = (f32[1,512]{1,0:T(1,128)S(1)}, f32[512,256]{1,0:T(8,128)}, f32[8,128]{1,0:T(8,128)}) custom-call(s32[1]{0:T(128)S(6)} %copy.35.live_ref, bf16[512,512]{1,0:T(8,128)(2,1)} %rows_ref.1, f32[1,512]{1,0:T(1,128)} %bitcast.45, s32[4,64]{1,0:T(4,128)} %pattern_ref.1, f32[512,512]{1,0:T(8,128)} %q_ref.1), custom_call_target="tpu_custom_call" | custom-call | tf_op jit(solution)/shard_map/pallas_call | solution.py:280
  121.5 1.2 slice.49
  123.3 0.6 copy.37
  123.9 1.9 %copy.38 = f32[512,256]{1,0:T(8,128)} copy(f32[512,256]{1,0:T(8,128)} %get-tuple-element.128) | data formatting | bytes 1048576
  (1 shorter events, 0.0 us)

commit v3 on v2

--- a/solution.py
+++ b/solution.py
@@ -65,15 +65,26 @@
         return later
 
     lax.fori_loop(0, steps, step, jnp.float32(grown * low))
-    resid = (eye() - dot(mh[...], xb[...])) - (dot(mm[...], xb[...]) + dot(ml[...], xb[...]))
-    rb[...] = resid.astype(BF16)
+
+
+def residual(m_ref, xb, rb, mh, mm):
+    m_ref[...] = (eye() - dot(xb[...], mh[...])) - dot(xb[...], mm[...])
+    rb[...] = m_ref[...].astype(BF16)
+
+
+def inverse_rows(m_ref, xb, rb, ml, start, count):
+    at = pl.ds(pl.multiple_of(start, 16), count)
+    x_rows = xb[at, :]
+    t = (m_ref[at, :] - dot(x_rows, ml[...])) + dot(rb[at, :], rb[...])
+    both = dot(jnp.concatenate(split(t), axis=0), xb[...])
+    return x_rows.astype(F32) + (both[:count] + both[count:])
+
+
+def inverse_whole(m_ref, xb, rb, mh, ml):
     square = dot(rb[...], rb[...])
-    rb[...], mh[...] = split(resid + square)
-    return jnp.sum(square * square, keepdims=True)
-
-
-def finish(out_ref, xb, rb, mh):
-    out_ref[...] = xb[...].astype(F32) + (dot(xb[...], rb[...]) + dot(xb[...], mh[...]))
+    rb[...], mh[...] = split((m_ref[...] - dot(xb[...], ml[...])) + square)
+    whole = xb[...].astype(F32) + (dot(rb[...], xb[...]) + dot(mh[...], xb[...]))
+    return whole, jnp.sum(square * square, keepdims=True)
 
 
 def mm3_row(values, right):
@@ -99,105 +110,7 @@
     return leaf - mine * stride + ((mine + k) % 4) * stride
 
 
-PARTNER = 21
-SEMS = PARTNER + 8
-
-
-def exchange(tier, g_ref, w_ref, parts, vecs, full, u_ref, send_sems, recv_sems, sent, meanwhile):
-    leaf, core = lax.axis_index("leaf"), lax.axis_index("blk")
-    z, y, x = place(leaf)
-    mine, stride = group(tier, leaf)
-    gather_y = tier >= 2
-    eighth = N // 8
-
-    def quarter(c, x_at):
-        return pl.ds(pl.multiple_of(c * HALF + x_at * eighth, eighth), eighth)
-
-    def cols(h):
-        return pl.ds(h * HALF, HALF)
-
-    def remote(src, dst, index, device):
-        copy = pltpu.make_async_remote_copy(
-            src_ref=src, dst_ref=dst, send_sem=send_sems.at[tier, index], recv_sem=recv_sems.at[tier, index],
-            device_id=device, device_id_type=MESH,
-        )
-        copy.start()
-        sent.append(copy)
-        return copy
-
-    def spread(rows, h, start, mine, stride):
-        part = full.at[tier, rows, cols(h)]
-        return [remote(part, part, start + 3 * h + k - 1, (ring(leaf, mine, stride, k), core)) for k in (1, 2, 3)]
-
-    own = quarter(core, x)
-    if gather_y:
-        own = pl.ds(pl.multiple_of(core * HALF + x * eighth + y * 16, 16), 16)
-    first = [[], []]
-    for h in (0, 1):
-        for k in (1, 2, 3):
-            source = quarter(core, (x + k) % 4) if tier == 0 else own
-            first[h].append(
-                remote(
-                    g_ref.at[source, cols(h)], parts.at[mine, :, cols(h)], 3 * h + k - 1,
-                    (ring(leaf, mine, stride, k), core),
-                )
-            )
-        if h == 0:
-            vectors = [
-                remote(w_ref, vecs.at[tier, mine], 5 + k, (ring(leaf, mine, stride, k), core)) for k in (1, 2, 3)
-            ]
-    parts[mine, :, :] = g_ref[own, :]
-    vecs[tier, mine] = w_ref[...]
-    meanwhile()
-    along_y, along_x, halves = [], [], []
-
-    def to_x(h):
-        along_x.append(spread(quarter(core, x), h, 15, x, 1))
-        to_partner(h, 0)
-
-    def to_partner(h, k):
-        part = full.at[tier, quarter(core, (x + 4 - k) % 4), cols(h)]
-        halves.append(remote(part, part, PARTNER + 4 * h + k, (leaf, 1 - core)))
-
-    for h in (0, 1):
-        for copy in first[h]:
-            copy.wait_recv()
-        at = slice(h * HALF, (h + 1) * HALF)
-        full[tier, own, at] = (parts[0, :, at] + parts[1, :, at]) + (parts[2, :, at] + parts[3, :, at])
-        if gather_y:
-            along_y.append(spread(own, h, 9, y, 4))
-        else:
-            to_x(h)
-    for h in (0, 1):
-        if gather_y:
-            for copy in along_y[h]:
-                copy.wait_recv()
-            to_x(h)
-    for copy in vectors:
-        copy.wait_recv()
-    u_ref[...] = (vecs[tier, 0] + vecs[tier, 1]) + (vecs[tier, 2] + vecs[tier, 3])
-    for h in (0, 1):
-        for k in (1, 3, 2):
-            along_x[h][k - 1].wait_recv()
-            to_partner(h, k)
-    for copy in halves:
-        copy.wait_recv()
-
-
-def smoother_kernel(
-    live_ref, rows_ref, values_ref, pattern_ref, q_ref, mean_ref, cov_ref, missed_ref,
-    g, m_ref, xb, rb, mh, mm, ml, gh, gl, vh, vl, qh, ql, r, w, u_ref, full, vecs, parts0, parts1, parts2, parts3,
-    send_sems, recv_sems,
-):
-    leaf, core = lax.axis_index("leaf"), lax.axis_index("blk")
-    barrier = pltpu.get_barrier_semaphore()
-    for tier in range(4):
-        mine, stride = group(tier, leaf)
-        for k in (1, 2, 3):
-            peer = (ring(leaf, mine, stride, k), core)
-            pl.semaphore_signal(barrier, inc=1, device_id=peer, device_id_type=MESH)
-    pl.semaphore_signal(barrier, inc=1, device_id=(leaf, 1 - core), device_id_type=MESH)
-
+def observe(live_ref, rows_ref, values_ref, pattern_ref, q_ref):
     blocks, wide = pattern_ref.shape
     row_of = lax.broadcasted_iota(jnp.int32, (wide, N), 0)
     widen = (lax.broadcasted_iota(jnp.int32, (wide, N), 1) // (N // wide) == row_of).astype(F32)
@@ -207,63 +120,190 @@
     masked = jnp.concatenate(
         [rows_ref[i * size : (i + 1) * size, :] * keep[i : i + 1, :].astype(BF16) for i in range(blocks)], axis=0
     )
-    m = dot(masked, masked, ((0,), (0,))) + q_ref[...]
+    vector = mm3_row(jnp.broadcast_to(values_ref[...], (8, N)), masked)
+    return dot(masked, masked, ((0,), (0,))) + q_ref[...], vector
+
+
+VECTOR, PHASE_A, PHASE_B, PARTNER = 6, 9, 15, 21
+SEMS = PARTNER + 8
+
+
+def exchange(tier, send, w_ref, parts, vecs, full, u_ref, send_sems, recv_sems, sent, first_work, second_work):
+    leaf, core = lax.axis_index("leaf"), lax.axis_index("blk")
+    z, y, x = place(leaf)
+    mine, stride = group(tier, leaf)
+    strip = core * 4 + x
+    strips = pl.ds(core * 4, 4)
+
+    def cols(h):
+        return pl.ds(h * HALF, HALF)
+
+    def remote(src, dst, index, device):
+        copy = pltpu.make_async_remote_copy(
+            src_ref=src, dst_ref=dst, send_sem=send_sems.at[tier, index], recv_sem=recv_sems.at[tier, index],
+            device_id=device, device_id_type=MESH,
+        )
+        copy.start()
+        sent.append(copy)
+        return copy
+
+    def spread(part, start, mine, stride):
+        return [remote(part, part, start + k - 1, (ring(leaf, mine, stride, k), core)) for k in (1, 2, 3)]
+
+    def to_partner(h, j, part):
+        halves.append(remote(part, part, PARTNER + 4 * h + j, (leaf, 1 - core)))
+
+    first, halves = [[], []], []
+    for h in (0, 1):
+        for k in (1, 2, 3):
+            device = (ring(leaf, mine, stride, k), core)
+            if tier == 0:
+                src, dst = send.at[(mine + k) % 4, :, :, cols(h)], parts.at[mine, :, :, cols(h)]
+            elif tier == 1:
+                src, dst = send.at[(mine + k) % 4, :, cols(h)], parts.at[mine, :, cols(h)]
+            else:
+                src, dst = send.at[:, cols(h)], parts.at[mine, :, cols(h)]
+            first[h].append(remote(src, dst, 3 * h + k - 1, device))
+    parts[mine] = send[mine] if tier < 2 else send[...]
+    first_work()
+    vecs[tier, mine] = w_ref[...]
+    vectors = [
+        remote(w_ref, vecs.at[tier, mine], VECTOR + k - 1, (ring(leaf, mine, stride, k), core)) for k in (1, 2, 3)
+    ]
+    along = {}
+
+    def strip_part(h, number):
+        return full.at[tier, number, :, :, cols(h)]
+
+    def level_part(h, number):
+        return full.at[tier, strips, number, :, cols(h)]
+
+    for h in (0, 1):
+        for copy in first[h]:
+            copy.wait_recv()
+        at = slice(h * HALF, (h + 1) * HALF)
+        total = (parts[0, ..., at] + parts[1, ..., at]) + (parts[2, ..., at] + parts[3, ..., at])
+        if tier == 0:
+            full[tier, strip, :, :, at] = total
+            along[h] = spread(strip_part(h, strip), PHASE_B + 3 * h, x, 1)
+            to_partner(h, 0, strip_part(h, strip))
+        else:
+            full[tier, strip, y, :, at] = total
+            own = full.at[tier, strip, y, :, cols(h)]
+            along[h] = spread(own, PHASE_A, y, 4) if h == 0 else spread(own, PHASE_A + 3, x, 1)
+    second_work()
+    if tier > 0:
+        for copy in along[0]:
+            copy.wait_recv()
+        along[0] = spread(strip_part(0, strip), PHASE_B, x, 1)
+        for copy in along[1]:
+            copy.wait_recv()
+        along[1] = spread(level_part(1, y), PHASE_B + 3, y, 4)
+        to_partner(0, 0, strip_part(0, strip))
+        to_partner(1, 0, level_part(1, y))
+    for k in (1, 3, 2):
+        for h in (0, 1):
+            along[h][k - 1].wait_recv()
+            if tier == 0 or h == 0:
+                to_partner(h, k, strip_part(h, core * 4 + (x + 4 - k) % 4))
+            else:
+                to_partner(h, k, level_part(h, (y + 4 - k) % 4))
+    for copy in halves:
+        copy.wait_recv()
+    for copy in vectors:
+        copy.wait_recv()
+    u_ref[...] = (vecs[tier, 0] + vecs[tier, 1]) + (vecs[tier, 2] + vecs[tier, 3])
+
+
+def smoother_kernel(
+    live_ref, rows_ref, values_ref, pattern_ref, q_ref, mean_ref, near_ref, far_ref, missed_ref,
+    m_ref, xb, rb, mh, mm, ml, gh, gl, hh, hl, vector_ref, r, mean_acc, w, u_ref, full, vecs,
+    send0, send1, send2, send3, parts0, parts1, parts2, parts3, send_sems, recv_sems,
+):
+    leaf, core = lax.axis_index("leaf"), lax.axis_index("blk")
+    z, y, x = place(leaf)
+    barrier = pltpu.get_barrier_semaphore()
+    for tier in range(4):
+        mine, stride = group(tier, leaf)
+        for k in (1, 2, 3):
+            peer = (ring(leaf, mine, stride, k), core)
+            pl.semaphore_signal(barrier, inc=1, device_id=peer, device_id_type=MESH)
+    pl.semaphore_signal(barrier, inc=1, device_id=(leaf, 1 - core), device_id_type=MESH)
+
+    m, vector_ref[...] = observe(live_ref, rows_ref, values_ref, pattern_ref, q_ref)
     m_ref[...] = m
-    vector = mm3_row(jnp.broadcast_to(values_ref[...], (8, N)), masked)
     bound = jnp.max(jnp.sum(jnp.abs(m), axis=0, keepdims=True)) * 1.00001
-    missed = invert(m_ref, xb, rb, mh, mm, ml, 1.0 / bound, 1.0 / 64.0, 4)
-    v_ref = g.at[0]
-    finish(v_ref, xb, rb, mh)
-    vh[...], vl[...] = split(v_ref[...])
-    w[0] = flagged(mm3(split(vector), (vh[...], vl[...])), 0.0, missed)
+    invert(m_ref, xb, rb, mh, mm, ml, 1.0 / bound, 1.0 / 64.0, 4)
+    residual(m_ref, xb, rb, mh, mm)
+    send0[...] = inverse_rows(m_ref, xb, rb, ml, core * HALF, HALF).reshape(4, 4, 16, N)
     pl.semaphore_wait(barrier, 13)
 
-    half = pl.ds(pl.multiple_of(core * HALF, HALF), HALF)
+    def leaf_first():
+        v, missed = inverse_whole(m_ref, xb, rb, mh, ml)
+        gh[...], gl[...] = split(v)
+        w[0] = flagged(mm3(split(vector_ref[...]), (gh[...], gl[...])), 0.0, missed)
+        mean_acc[...] = w[0]
+        near_ref[...] = send0[...].reshape(HALF, N).T
+        r[...] = near_ref[...]
+
+    def leaf_second():
+        hh[...], hl[...] = split(mm3((gh[...], gl[...]), split(q_ref[...])))
+
+    def tier_first(n):
+        def work():
+            gain, missed = inverse_whole(m_ref, xb, rb, mh, ml)
+            gh[...], gl[...] = split(gain)
+            u = u_ref[...]
+            w[n] = flagged(mm3(split(u), (gh[...], gl[...]), NT), u, missed)
+
+        return work
+
+    def tier_second(n):
+        def work():
+            r[...] = mm3((gh[...], gl[...]), split(r[...]))
+            near_ref[...] += mm3((hh[...], hl[...]), split(r[...]))
+            mean_acc[...] += mm3(split(w[n]), (hh[...], hl[...]), NT)
+            hh[...], hl[...] = split(mm3((hh[...], hl[...]), (gh[...], gl[...])))
+
+        return work
+
+    sends = (send0, send1, send2, send3)
     parts = (parts0, parts1, parts2, parts3)
     sent = []
-
-    def meanwhile_leaf():
-        qh[...], ql[...] = split(q_ref[...])
-        r[0] = v_ref[:, half]
-
-    def meanwhile_tier(n):
-        def work():
-            r[n] = mm3((gh[n - 1], gl[n - 1]), split(r[n - 1]))
-
-        return work
-
     for tier in range(4):
         exchange(
-            tier, g.at[tier], w.at[tier], parts[tier], vecs, full, u_ref, send_sems, recv_sems, sent,
-            meanwhile_leaf if tier == 0 else meanwhile_tier(tier),
+            tier, sends[tier], w.at[tier], parts[tier], vecs, full, u_ref, send_sems, recv_sems, sent,
+            leaf_first if tier == 0 else tier_first(tier), leaf_second if tier == 0 else tier_second(tier),
         )
+        total = full[tier].reshape(N, N)
         if tier == 0:
-            m_ref[...] = 5.0 * eye() - mm6(split3(full[0]), split3(q_ref[...]))
+            m_ref[...] = 5.0 * eye() - mm6(split3(total), split3(q_ref[...]))
         else:
-            m_ref[...] = 5.0 * eye() - full[tier]
-        missed = invert(m_ref, xb, rb, mh, mm, ml, 1.0 / 5.001, 0.1999, 2)
-        u = u_ref[...]
+            m_ref[...] = 5.0 * eye() - total
+        invert(m_ref, xb, rb, mh, mm, ml, 1.0 / 5.001, 0.1999, 2)
         if tier < 3:
-            g_ref = g.at[tier + 1]
-            finish(g_ref, xb, rb, mh)
-            gh[tier], gl[tier] = split(g_ref[...])
-            w[tier + 1] = flagged(mm3(split(u), (gh[tier], gl[tier]), NT), u, missed)
-        else:
-            u = u + mm3(split(u), (rb[...], mh[...]), NT)
-            uh, ul = split(u)
-            mean = dot(uh, xb[...], NT) + dot(ul, xb[...], NT)
-            missed_ref[...] = (u_ref[1:2, 0:128] + jnp.where(missed < 4e-7, 0.0, 1.0)) * jnp.ones((8, 128), F32)
-            q = r[3] + mm3((rb[...], mh[...]), split(r[3]))
-            q_high, q_low = split(q)
-            q = dot(xb[...], q_high) + dot(xb[...], q_low)
-    for n in (3, 2, 1):
-        gain = (gh[n - 1], gl[n - 1])
-        q = r[n] + mm3(gain, split(q))
-        mean = w[n] + mm3(split(mean), gain, NT)
-    info = (qh[...], ql[...])
-    v = (vh[...], vl[...])
-    cov_ref[...] = r[0] + mm3(v, split(mm3(info, split(q))))
-    mean = w[0] + mm3(split(mm3(split(mean), info)), v)
+            residual(m_ref, xb, rb, mh, mm)
+        if tier == 0:
+            start = core * HALF + x * 64
+            send1[...] = inverse_rows(m_ref, xb, rb, ml, start, 64).reshape(4, 16, N)
+        elif tier < 3:
+            start = core * HALF + x * 64 + y * 16
+            sends[tier + 1][...] = inverse_rows(m_ref, xb, rb, ml, start, 16)
+    resid = (eye() - dot(mh[...], xb[...])) - (dot(mm[...], xb[...]) + dot(ml[...], xb[...]))
+    rb[...] = resid.astype(BF16)
+    square = dot(rb[...], rb[...])
+    rb[...], mh[...] = split(resid + square)
+    missed = jnp.where(jnp.sum(square * square, keepdims=True) < 4e-7, 0.0, 1.0)
+    missed_ref[0] = jnp.max(u_ref[1:2, 0:128] + missed)
+    q = r[...] + mm3((rb[...], mh[...]), split(r[...]))
+    q_high, q_low = split(q)
+    q = dot(xb[...], q_high) + dot(xb[...], q_low)
+    far_ref[...] = mm3((hh[...], hl[...]), split(q))
+    u = u_ref[...]
+    u = u + mm3(split(u), (rb[...], mh[...]), NT)
+    u_high, u_low = split(u)
+    mean = dot(u_high, xb[...], NT) + dot(u_low, xb[...], NT)
+    mean = mean_acc[...] + mm3(split(mean), (hh[...], hl[...]), NT)
     mean_ref[...] = mean[0:1, :]
     for copy in sent:
         copy.wait_send()
@@ -274,19 +314,21 @@
 
 
 def smoother(obs_rows, obs_values, track_blocks, pattern, process_info):
-    def square(count, dtype):
-        return pltpu.VMEM((count, N, N) if count > 1 else (N, N), dtype)
-
+    def square(dtype):
+        return pltpu.VMEM((N, N), dtype)
+
+    vector = pltpu.VMEM((8, N), F32)
+    pieces = [(4, 16, N), (16, N), (16, N), (16, N)]
+    sends = [(4, 4, 16, N), (4, 16, N), (16, N), (16, N)]
     return pl.pallas_call(
         smoother_kernel,
-        out_shape=(matrix(1), matrix(N, HALF), matrix(8, 128)),
+        out_shape=(matrix(1), matrix(N, HALF), matrix(N, HALF), jax.ShapeDtypeStruct((1,), F32)),
         in_specs=[SMEM_SPEC] + [VMEM_SPEC] * 4,
-        out_specs=(VMEM_SPEC,) * 3,
+        out_specs=(VMEM_SPEC,) * 3 + (SMEM_SPEC,),
         scratch_shapes=[
-            square(4, F32), square(1, F32), *[square(1, BF16)] * 5, square(3, BF16), square(3, BF16), *[square(1, BF16)] * 4,
-            pltpu.VMEM((4, N, HALF), F32), pltpu.VMEM((4, 8, N), F32), pltpu.VMEM((8, N), F32), square(4, F32),
-            pltpu.VMEM((4, 4, 8, N), F32),
-            *[pltpu.VMEM((4, rows, N), F32) for rows in (64, 64, 16, 16)],
+            square(F32), *[square(BF16)] * 9, vector, pltpu.VMEM((N, HALF), F32), vector, pltpu.VMEM((4, 8, N), F32), vector,
+            pltpu.VMEM((4, 8, 4, 16, N), F32), pltpu.VMEM((4, 4, 8, N), F32),
+            *[pltpu.VMEM(shape, F32) for shape in sends], *[pltpu.VMEM((4, *shape), F32) for shape in pieces],
             pltpu.SemaphoreType.DMA((4, SEMS)), pltpu.SemaphoreType.DMA((4, SEMS)),
         ],
         compiler_params=pltpu.CompilerParams(vmem_limit_bytes=LIMIT, collective_id=0, has_side_effects=True),
@@ -482,18 +524,24 @@
     )(g, w)
 
 
+def careful_leaf_kernel(live_ref, rows_ref, values_ref, pattern_ref, q_ref, m_ref, vector_ref):
+    m_ref[...], vector_ref[...] = observe(live_ref, rows_ref, values_ref, pattern_ref, q_ref)
+
+
 def careful(obs_rows, obs_values, track_blocks, pattern, process_info):
-    blocks, wide = pattern.shape
-    keep = jnp.repeat(pattern.astype(BF16), N // wide, axis=1)
-    keep = keep * (jnp.arange(blocks) < track_blocks[0]).astype(BF16)[:, None]
-    masked = (obs_rows.reshape(blocks, -1, N) * keep[:, None, :]).reshape(-1, N)
-    m = jnp.dot(masked.T, masked, preferred_element_type=F32) + process_info
+    m, vector = pl.pallas_call(
+        careful_leaf_kernel,
+        out_shape=(matrix(), matrix(8)),
+        in_specs=[SMEM_SPEC] + [VMEM_SPEC] * 4,
+        out_specs=(VMEM_SPEC,) * 2,
+        compiler_params=pltpu.CompilerParams(vmem_limit_bytes=LIMIT),
+    )(track_blocks, obs_rows, obs_values[None, :], pattern, process_info)
     v = careful_inverse(m, 1.0 / (jnp.max(jnp.sum(jnp.abs(m), axis=0)) * 1.00001))
 
     def column(vector):
         return jnp.broadcast_to(vector[:, None], (N, 128))
 
-    w0 = careful_product(v, careful_product(masked.T.astype(F32), column(obs_values)))
+    w0 = careful_product(v, column(vector[0]))
     g, w = v, w0
     r0 = lax.dynamic_slice_in_dim(v, lax.axis_index("blk") * HALF, HALF, 1)
     r, gains, kept = r0, [], []
@@ -517,8 +565,14 @@
 
 
 def shards(*args):
-    mean, cov, missed = smoother(*args)
-    return lax.cond(missed[0, 0] > 0.5, lambda: careful(*args), lambda: (mean, cov))
+    mean, near, far, missed = smoother(*args)
+
+    def again(state):
+        mean, cov = careful(*args)
+        return mean, cov, jnp.zeros_like(cov), jnp.zeros_like(missed)
+
+    mean, near, far, missed = lax.while_loop(lambda state: state[3][0] > 0.5, again, (mean, near, far, missed))
+    return mean, near + far
 
 
 def solution(mesh):

time: 126 us -> 114 us (0.905)
  Pallas kernels: 120 us -> 108 us
  local copies, waits for them, and re-layouts: 3.64 us -> 1.24 us
  other arithmetic: 0 us -> 2.06 us
    pallas_call x1, Pallas kernels: 120 us -> 108 us  [smoother(): pl.pallas_call(smoother_kernel, out_shape=(matrix(1), matrix(N, HALF), ma...]
    add x0 -> x1, other arithmetic: none -> 2.06 us  [shards(): return (mean, near + far)]
where the time goes in v3:
time: 114 us
  Pallas kernels  108 us (95%)
  other arithmetic  2.06 us (2%)
  between operations  1.29 us (1%)
  local copies, waits for them, and re-layouts  1.24 us (1%)
    pallas_call x1, Pallas kernels, smoother(): pl.pallas_call(smoother_kernel, out_shape=(matrix(1), matrix(N, HALF), ma...  108 us

profile of v3, /device:TPU:1, one launch (start us, length us, event | category | flops | bytes accessed | tf_op | source)
XLA Modules:
  0.0 113.7 jit_solution(11497061280089117009)
XLA Ops:
  1.3 108.4 %shard_map.68 = (f32[1,512]{1,0:T(1,128)}, f32[512,256]{1,0:T(8,128)}, f32[512,256]{1,0:T(8,128)}, f32[1]{0:T(128)}) custom-call(s32[1]{0:T(128)S(6)} %copy.28.live_ref, bf16[512,512]{1,0:T(8,128)(2,1)} %rows_ref.1, f32[1,512]{1,0:T(1,128)} %bitcast.35, s32[4,64]{1,0:T(4,128)} %pattern_ref.1, f32[512,512]{1,0:T(8,128)} %q_ref.1), custom_call_target="tpu_custom_call" | custom-call | tf_op jit(solution)/shard_map/pallas_call | solution.py:323
  109.7 0.7 while.22
  110.4 2.1 %add.28 = f32[512,256]{1,0:T(8,128)} add(f32[512,256]{1,0:T(8,128)} %get-tuple-element.88, f32[512,256]{1,0:T(8,128)} %get-tuple-element.89) | non-fusion elementwise | flops 131072 | bytes 1572864 | tf_op jit(solution)/shard_map/add | solution.py:575
  112.5 1.2 %copy.31 = f32[1,512]{1,0:T(1,128)} copy(f32[1,512]{1,0:T(1,128)} %get-tuple-element.194) | data formatting | bytes 4096

commit v4 on v3

--- a/solution.py
+++ b/solution.py
@@ -72,10 +72,13 @@
     rb[...] = m_ref[...].astype(BF16)
 
 
-def inverse_rows(m_ref, xb, rb, ml, start, count):
-    at = pl.ds(pl.multiple_of(start, 16), count)
-    x_rows = xb[at, :]
-    t = (m_ref[at, :] - dot(x_rows, ml[...])) + dot(rb[at, :], rb[...])
+def inverse_rows(m_ref, xb, rb, ml, starts, size):
+    def rows_of(ref):
+        return jnp.concatenate([ref[pl.ds(pl.multiple_of(start, 16), size), :] for start in starts], axis=0)
+
+    count = len(starts) * size
+    x_rows = rows_of(xb)
+    t = (rows_of(m_ref) - dot(x_rows, ml[...])) + dot(rows_of(rb), rb[...])
     both = dot(jnp.concatenate(split(t), axis=0), xb[...])
     return x_rows.astype(F32) + (both[:count] + both[count:])
 
@@ -125,19 +128,13 @@
 
 
 VECTOR, PHASE_A, PHASE_B, PARTNER = 6, 9, 15, 21
-SEMS = PARTNER + 8
-
-
-def exchange(tier, send, w_ref, parts, vecs, full, u_ref, send_sems, recv_sems, sent, first_work, second_work):
-    leaf, core = lax.axis_index("leaf"), lax.axis_index("blk")
-    z, y, x = place(leaf)
-    mine, stride = group(tier, leaf)
-    strip = core * 4 + x
-    strips = pl.ds(core * 4, 4)
-
-    def cols(h):
-        return pl.ds(h * HALF, HALF)
-
+SYM_VECTOR, SYM_GATHER, SYM_PARTNER = 9, 12, 21
+SEMS = SYM_PARTNER + 12
+BLOCK = N // 4
+LAST = 256
+
+
+def sender(tier, send_sems, recv_sems, sent):
     def remote(src, dst, index, device):
         copy = pltpu.make_async_remote_copy(
             src_ref=src, dst_ref=dst, send_sem=send_sems.at[tier, index], recv_sem=recv_sems.at[tier, index],
@@ -147,6 +144,74 @@
         sent.append(copy)
         return copy
 
+    return remote
+
+
+def exchange_leaves(send, w_ref, parts, vecs, full, u_ref, send_sems, recv_sems, sent, first_work, second_work):
+    leaf, core = lax.axis_index("leaf"), lax.axis_index("blk")
+    z, y, x = place(leaf)
+    remote = sender(0, send_sems, recv_sems, sent)
+
+    def cols(owner, j):
+        return pl.ds(pl.multiple_of((owner + j) % 4 * BLOCK, BLOCK), BLOCK)
+
+    def near(k):
+        return ring(leaf, x, 1, k), core
+
+    first = [[], [], []]
+    for j in range(3):
+        for k in (1, 2, 3):
+            owner = (x + k) % 4
+            part = cols(owner, j)
+            first[j].append(remote(send.at[owner, :, :, part], parts.at[x, :, :, part], 3 * j + k - 1, near(k)))
+    parts[x] = send[x]
+    first_work()
+    vecs[0, x] = w_ref[...]
+    vectors = [remote(w_ref, vecs.at[0, x], SYM_VECTOR + k - 1, near(k)) for k in (1, 2, 3)]
+    gather, halves = [], []
+
+    def piece(owner, j):
+        return full.at[0, 2 * owner + core, :, :, cols(owner, j)]
+
+    def to_partner(k, j):
+        part = piece((x + 4 - k) % 4, j)
+        halves.append(remote(part, part, SYM_PARTNER + 3 * k + j, (leaf, 1 - core)))
+
+    for j in range(3):
+        for copy in first[j]:
+            copy.wait_recv()
+        at = cols(x, j)
+        full[0, 2 * x + core, :, :, at] = (parts[0, :, :, at] + parts[1, :, :, at]) + (parts[2, :, :, at] + parts[3, :, :, at])
+        part = piece(x, j)
+        gather.append([remote(part, part, SYM_GATHER + 3 * j + k - 1, near(k)) for k in (1, 2, 3)])
+        to_partner(0, j)
+    second_work()
+    for j in range(3):
+        for k in (1, 3, 2):
+            gather[j][k - 1].wait_recv()
+            to_partner(k, j)
+    for copy in halves:
+        copy.wait_recv()
+    for copy in vectors:
+        copy.wait_recv()
+    u_ref[...] = (vecs[0, 0] + vecs[0, 1]) + (vecs[0, 2] + vecs[0, 3])
+    for row in range(4):
+        col = (row + 3) % 4
+        block = full[0, 2 * col : 2 * col + 2, :, :, row * BLOCK : (row + 1) * BLOCK].reshape(BLOCK, BLOCK)
+        full[0, 2 * row : 2 * row + 2, :, :, col * BLOCK : (col + 1) * BLOCK] = block.T.reshape(2, 4, 16, BLOCK)
+
+
+def exchange(tier, send, w_ref, parts, vecs, full, u_ref, send_sems, recv_sems, sent, first_work, second_work):
+    leaf, core = lax.axis_index("leaf"), lax.axis_index("blk")
+    z, y, x = place(leaf)
+    mine, stride = group(tier, leaf)
+    strip = core * 4 + x
+    strips = pl.ds(core * 4, 4)
+    remote = sender(tier, send_sems, recv_sems, sent)
+
+    def cols(h):
+        return pl.ds(h * HALF, HALF)
+
     def spread(part, start, mine, stride):
         return [remote(part, part, start + k - 1, (ring(leaf, mine, stride, k), core)) for k in (1, 2, 3)]
 
@@ -156,58 +221,47 @@
     first, halves = [[], []], []
     for h in (0, 1):
         for k in (1, 2, 3):
+            src = send.at[(mine + k) % 4, :, cols(h)] if tier == 1 else send.at[:, cols(h)]
             device = (ring(leaf, mine, stride, k), core)
-            if tier == 0:
-                src, dst = send.at[(mine + k) % 4, :, :, cols(h)], parts.at[mine, :, :, cols(h)]
-            elif tier == 1:
-                src, dst = send.at[(mine + k) % 4, :, cols(h)], parts.at[mine, :, cols(h)]
-            else:
-                src, dst = send.at[:, cols(h)], parts.at[mine, :, cols(h)]
-            first[h].append(remote(src, dst, 3 * h + k - 1, device))
-    parts[mine] = send[mine] if tier < 2 else send[...]
+            first[h].append(remote(src, parts.at[mine, :, cols(h)], 3 * h + k - 1, device))
+    parts[mine] = send[mine] if tier == 1 else send[...]
     first_work()
     vecs[tier, mine] = w_ref[...]
     vectors = [
         remote(w_ref, vecs.at[tier, mine], VECTOR + k - 1, (ring(leaf, mine, stride, k), core)) for k in (1, 2, 3)
     ]
-    along = {}
-
-    def strip_part(h, number):
-        return full.at[tier, number, :, :, cols(h)]
-
-    def level_part(h, number):
-        return full.at[tier, strips, number, :, cols(h)]
+    if tier == 3:
+        second_work()
+    along = []
+
+    def strip_part(number):
+        return full.at[tier, number, :, :, cols(0)]
+
+    def level_part(number):
+        return full.at[tier, strips, number, :, cols(1)]
 
     for h in (0, 1):
         for copy in first[h]:
             copy.wait_recv()
         at = slice(h * HALF, (h + 1) * HALF)
-        total = (parts[0, ..., at] + parts[1, ..., at]) + (parts[2, ..., at] + parts[3, ..., at])
-        if tier == 0:
-            full[tier, strip, :, :, at] = total
-            along[h] = spread(strip_part(h, strip), PHASE_B + 3 * h, x, 1)
-            to_partner(h, 0, strip_part(h, strip))
-        else:
-            full[tier, strip, y, :, at] = total
-            own = full.at[tier, strip, y, :, cols(h)]
-            along[h] = spread(own, PHASE_A, y, 4) if h == 0 else spread(own, PHASE_A + 3, x, 1)
-    second_work()
-    if tier > 0:
-        for copy in along[0]:
-            copy.wait_recv()
-        along[0] = spread(strip_part(0, strip), PHASE_B, x, 1)
-        for copy in along[1]:
-            copy.wait_recv()
-        along[1] = spread(level_part(1, y), PHASE_B + 3, y, 4)
-        to_partner(0, 0, strip_part(0, strip))
-        to_partner(1, 0, level_part(1, y))
+        full[tier, strip, y, :, at] = (parts[0, :, at] + parts[1, :, at]) + (parts[2, :, at] + parts[3, :, at])
+        own = full.at[tier, strip, y, :, cols(h)]
+        along.append(spread(own, PHASE_A, y, 4) if h == 0 else spread(own, PHASE_A + 3, x, 1))
+    for copy in along[0]:
+        copy.wait_recv()
+    by_x = spread(strip_part(strip), PHASE_B, x, 1)
+    for copy in along[1]:
+        copy.wait_recv()
+    by_y = spread(level_part(y), PHASE_B + 3, y, 4)
+    to_partner(0, 0, strip_part(strip))
+    to_partner(1, 0, level_part(y))
+    if tier < 3:
+        second_work()
     for k in (1, 3, 2):
-        for h in (0, 1):
-            along[h][k - 1].wait_recv()
-            if tier == 0 or h == 0:
-                to_partner(h, k, strip_part(h, core * 4 + (x + 4 - k) % 4))
-            else:
-                to_partner(h, k, level_part(h, (y + 4 - k) % 4))
+        by_x[k - 1].wait_recv()
+        to_partner(0, k, strip_part(core * 4 + (x + 4 - k) % 4))
+        by_y[k - 1].wait_recv()
+        to_partner(1, k, level_part((y + 4 - k) % 4))
     for copy in halves:
         copy.wait_recv()
     for copy in vectors:
@@ -216,8 +270,8 @@
 
 
 def smoother_kernel(
-    live_ref, rows_ref, values_ref, pattern_ref, q_ref, mean_ref, near_ref, far_ref, missed_ref,
-    m_ref, xb, rb, mh, mm, ml, gh, gl, hh, hl, vector_ref, r, mean_acc, w, u_ref, full, vecs,
+    live_ref, rows_ref, values_ref, pattern_ref, q_ref, near_ref, q_out, hh, hl, mean_acc, mean_ref, missed_ref,
+    m_ref, xb, rb, mh, mm, ml, gh, gl, vector_ref, r, w, u_ref, full, vecs,
     send0, send1, send2, send3, parts0, parts1, parts2, parts3, send_sems, recv_sems,
 ):
     leaf, core = lax.axis_index("leaf"), lax.axis_index("blk")
@@ -235,7 +289,8 @@
     bound = jnp.max(jnp.sum(jnp.abs(m), axis=0, keepdims=True)) * 1.00001
     invert(m_ref, xb, rb, mh, mm, ml, 1.0 / bound, 1.0 / 64.0, 4)
     residual(m_ref, xb, rb, mh, mm)
-    send0[...] = inverse_rows(m_ref, xb, rb, ml, core * HALF, HALF).reshape(4, 4, 16, N)
+    starts = [i * BLOCK + core * 64 for i in range(4)]
+    send0[...] = inverse_rows(m_ref, xb, rb, ml, starts, 64).reshape(4, 4, 16, N)
     pl.semaphore_wait(barrier, 13)
 
     def leaf_first():
@@ -243,7 +298,8 @@
         gh[...], gl[...] = split(v)
         w[0] = flagged(mm3(split(vector_ref[...]), (gh[...], gl[...])), 0.0, missed)
         mean_acc[...] = w[0]
-        near_ref[...] = send0[...].reshape(HALF, N).T
+        m_ref[...] = v
+        near_ref[...] = m_ref[:, pl.ds(pl.multiple_of(core * HALF, HALF), HALF)]
         r[...] = near_ref[...]
 
     def leaf_second():
@@ -271,10 +327,11 @@
     parts = (parts0, parts1, parts2, parts3)
     sent = []
     for tier in range(4):
-        exchange(
-            tier, sends[tier], w.at[tier], parts[tier], vecs, full, u_ref, send_sems, recv_sems, sent,
-            leaf_first if tier == 0 else tier_first(tier), leaf_second if tier == 0 else tier_second(tier),
-        )
+        shared = (sends[tier], w.at[tier], parts[tier], vecs, full, u_ref, send_sems, recv_sems, sent)
+        if tier == 0:
+            exchange_leaves(*shared, leaf_first, leaf_second)
+        else:
+            exchange(tier, *shared, tier_first(tier), tier_second(tier))
         total = full[tier].reshape(N, N)
         if tier == 0:
             m_ref[...] = 5.0 * eye() - mm6(split3(total), split3(q_ref[...]))
@@ -285,10 +342,10 @@
             residual(m_ref, xb, rb, mh, mm)
         if tier == 0:
             start = core * HALF + x * 64
-            send1[...] = inverse_rows(m_ref, xb, rb, ml, start, 64).reshape(4, 16, N)
+            send1[...] = inverse_rows(m_ref, xb, rb, ml, [start], 64).reshape(4, 16, N)
         elif tier < 3:
             start = core * HALF + x * 64 + y * 16
-            sends[tier + 1][...] = inverse_rows(m_ref, xb, rb, ml, start, 16)
+            sends[tier + 1][...] = inverse_rows(m_ref, xb, rb, ml, [start], 16)
     resid = (eye() - dot(mh[...], xb[...])) - (dot(mm[...], xb[...]) + dot(ml[...], xb[...]))
     rb[...] = resid.astype(BF16)
     square = dot(rb[...], rb[...])
@@ -297,14 +354,11 @@
     missed_ref[0] = jnp.max(u_ref[1:2, 0:128] + missed)
     q = r[...] + mm3((rb[...], mh[...]), split(r[...]))
     q_high, q_low = split(q)
-    q = dot(xb[...], q_high) + dot(xb[...], q_low)
-    far_ref[...] = mm3((hh[...], hl[...]), split(q))
+    q_out[...] = dot(xb[...], q_high) + dot(xb[...], q_low)
     u = u_ref[...]
     u = u + mm3(split(u), (rb[...], mh[...]), NT)
     u_high, u_low = split(u)
-    mean = dot(u_high, xb[...], NT) + dot(u_low, xb[...], NT)
-    mean = mean_acc[...] + mm3(split(mean), (hh[...], hl[...]), NT)
-    mean_ref[...] = mean[0:1, :]
+    mean_ref[...] = dot(u_high, xb[...], NT) + dot(u_low, xb[...], NT)
     for copy in sent:
         copy.wait_send()
 
@@ -322,17 +376,47 @@
     sends = [(4, 4, 16, N), (4, 16, N), (16, N), (16, N)]
     return pl.pallas_call(
         smoother_kernel,
-        out_shape=(matrix(1), matrix(N, HALF), matrix(N, HALF), jax.ShapeDtypeStruct((1,), F32)),
+        out_shape=(
+            matrix(N, HALF), matrix(N, HALF), matrix(dtype=BF16), matrix(dtype=BF16), matrix(8), matrix(8),
+            jax.ShapeDtypeStruct((1,), F32),
+        ),
         in_specs=[SMEM_SPEC] + [VMEM_SPEC] * 4,
-        out_specs=(VMEM_SPEC,) * 3 + (SMEM_SPEC,),
+        out_specs=(VMEM_SPEC,) * 6 + (SMEM_SPEC,),
         scratch_shapes=[
-            square(F32), *[square(BF16)] * 9, vector, pltpu.VMEM((N, HALF), F32), vector, pltpu.VMEM((4, 8, N), F32), vector,
+            square(F32), *[square(BF16)] * 7, vector, pltpu.VMEM((N, HALF), F32), pltpu.VMEM((4, 8, N), F32), vector,
             pltpu.VMEM((4, 8, 4, 16, N), F32), pltpu.VMEM((4, 4, 8, N), F32),
             *[pltpu.VMEM(shape, F32) for shape in sends], *[pltpu.VMEM((4, *shape), F32) for shape in pieces],
             pltpu.SemaphoreType.DMA((4, SEMS)), pltpu.SemaphoreType.DMA((4, SEMS)),
         ],
         compiler_params=pltpu.CompilerParams(vmem_limit_bytes=LIMIT, collective_id=0, has_side_effects=True),
     )(track_blocks, obs_rows, obs_values[None, :], pattern, process_info)
+
+
+def last_kernel(near_ref, q_ref, hh_ref, hl_ref, mean_acc_ref, mean_ref, cov_out, mean_out):
+    h = (hh_ref[...], hl_ref[...])
+    cov_out[...] = near_ref[...] + mm3(h, split(q_ref[...]))
+    mean = mean_acc_ref[...] + mm3(split(mean_ref[...]), h, NT)
+    mean_out[...] = mean[0:1, :]
+
+
+def last(near, q, hh, hl, mean_acc, mean):
+    def rows(cols):
+        return pl.BlockSpec((LAST, cols), lambda i: (i, 0))
+
+    def lanes(count):
+        return pl.BlockSpec((count, LAST), lambda i: (0, i))
+
+    def whole(count, cols):
+        return pl.BlockSpec((count, cols), lambda i: (0, 0))
+
+    return pl.pallas_call(
+        last_kernel,
+        out_shape=(matrix(N, HALF), matrix(1)),
+        grid=(N // LAST,),
+        in_specs=[rows(HALF), whole(N, HALF), rows(N), rows(N), lanes(8), whole(8, N)],
+        out_specs=(rows(HALF), lanes(1)),
+        compiler_params=pltpu.CompilerParams(vmem_limit_bytes=LIMIT),
+    )(near, q, hh, hl, mean_acc, mean)
 
 
 ROWS = 64
@@ -565,14 +649,15 @@
 
 
 def shards(*args):
-    mean, near, far, missed = smoother(*args)
+    *pieces, missed = smoother(*args)
+    cov, mean = last(*pieces)
 
     def again(state):
         mean, cov = careful(*args)
-        return mean, cov, jnp.zeros_like(cov), jnp.zeros_like(missed)
-
-    mean, near, far, missed = lax.while_loop(lambda state: state[3][0] > 0.5, again, (mean, near, far, missed))
-    return mean, near + far
+        return mean, cov, jnp.zeros_like(missed)
+
+    mean, cov, missed = lax.while_loop(lambda state: state[2][0] > 0.5, again, (mean, cov, missed))
+    return mean, cov
 
 
 def solution(mesh):

time: 114 us -> 110 us (0.965)
  other arithmetic: 2.06 us -> 0 us
  local copies, waits for them, and re-layouts: 1.24 us -> 0.01 us
    add x1 -> x0, other arithmetic: 2.06 us -> none  [shards(): return (mean, near + far)]
    unnamed x1 -> x4, local copies, waits for them, and re-layouts: 1.24 us -> 0.01 us
    pallas_call x1 -> x2, Pallas kernels: 108 us -> 108 us  [the longest x1 105 us: smoother(): pl.pallas_call(smoother_kernel, out_shape=(matrix(N, HALF), matrix(N, HAL...]
where the time goes in v4:
time: 110 us
  Pallas kernels  108 us (98%)
  between operations  1.51 us (1%)
    pallas_call x1, Pallas kernels, smoother(): pl.pallas_call(smoother_kernel, out_shape=(matrix(N, HALF), matrix(N, HAL...  105 us
    pallas_call x1, Pallas kernels, last(): pl.pallas_call(last_kernel, out_shape=(matrix(N, HALF), matrix(1)), grid=...  3.27 us

profile of v4, /device:TPU:1, one launch (start us, length us, event | category | flops | bytes accessed | tf_op | source)
XLA Modules:
  0.0 110.0 jit_solution(4164646431096220163)
XLA Ops:
  0.6 0.0 copy-start.8
  0.6 0.0 copy-start.9
  1.3 104.6 %shard_map.68 = (f32[512,256]{1,0:T(8,128)}, f32[512,256]{1,0:T(8,128)}, bf16[512,512]{1,0:T(8,128)(2,1)}, bf16[512,512]{1,0:T(8,128)(2,1)}, f32[8,512]{1,0:T(8,128)}, /*index=5*/f32[8,512]{1,0:T(8,128)}, f32[1]{0:T(128)}) custom-call(s32[1]{0:T(128)S(6)} %copy.24.live_ref, bf16[512,512]{1,0:T(8,128)(2,1)} %rows_ref.1, f32[1,512]{1,0:T(1,128)} %bitcast.35, ...), custom_call_target="tpu_custom_call" | custom-call | tf_op jit(solution)/shard_map/pallas_call | solution.py:377
  105.9 3.3 %shard_map.69 = (f32[512,256]{1,0:T(8,128)}, f32[1,512]{1,0:T(1,128)}) custom-call(f32[512,256]{1,0:T(8,128)} %get-tuple-element.83.near_ref, f32[512,256]{1,0:T(8,128)} %get-tuple-element.84.q_ref, bf16[512,512]{1,0:T(8,128)(2,1)} %get-tuple-element.85.hh_ref, bf16[512,512]{1,0:T(8,128)(2,1)} %get-tuple-element.86.hl_ref, ...), custom_call_target="tpu_custom_call" | custom-call | tf_op jit(solution)/shard_map/pallas_call | solution.py:412
  109.2 0.0 copy-done.8
  109.2 0.0 copy-done.9
  109.2 0.6 while.20
Async XLA Ops:
  0.6 108.6 %copy-start.8 = (f32[512]{0:T(512)S(1)}, f32[512]{0:T(512)}, u32[]{:S(2)}) copy-start(f32[512]{0:T(512)} %param.10) | copy-start | bytes 6148
  0.6 108.6 %copy-start.9 = (s32[4,64]{1,0:T(4,128)S(1)}, s32[4,64]{1,0:T(4,128)}, u32[]{:S(2)}) copy-start(s32[4,64]{1,0:T(4,128)} %pattern_ref.1) | copy-start | bytes 3076

commit v5 on v4

--- a/solution.py
+++ b/solution.py
@@ -113,7 +113,7 @@
     return leaf - mine * stride + ((mine + k) % 4) * stride
 
 
-def observe(live_ref, rows_ref, values_ref, pattern_ref, q_ref):
+def observe(live_ref, rows_ref, pattern_ref):
     blocks, wide = pattern_ref.shape
     row_of = lax.broadcasted_iota(jnp.int32, (wide, N), 0)
     widen = (lax.broadcasted_iota(jnp.int32, (wide, N), 1) // (N // wide) == row_of).astype(F32)
@@ -123,8 +123,7 @@
     masked = jnp.concatenate(
         [rows_ref[i * size : (i + 1) * size, :] * keep[i : i + 1, :].astype(BF16) for i in range(blocks)], axis=0
     )
-    vector = mm3_row(jnp.broadcast_to(values_ref[...], (8, N)), masked)
-    return dot(masked, masked, ((0,), (0,))) + q_ref[...], vector
+    return masked
 
 
 VECTOR, PHASE_A, PHASE_B, PARTNER = 6, 9, 15, 21
@@ -160,7 +159,7 @@
 
     first = [[], [], []]
     for j in range(3):
-        for k in (1, 2, 3):
+        for k in (2, 1, 3):
             owner = (x + k) % 4
             part = cols(owner, j)
             first[j].append(remote(send.at[owner, :, :, part], parts.at[x, :, :, part], 3 * j + k - 1, near(k)))
@@ -220,7 +219,7 @@
 
     first, halves = [[], []], []
     for h in (0, 1):
-        for k in (1, 2, 3):
+        for k in (2, 1, 3):
             src = send.at[(mine + k) % 4, :, cols(h)] if tier == 1 else send.at[:, cols(h)]
             device = (ring(leaf, mine, stride, k), core)
             first[h].append(remote(src, parts.at[mine, :, cols(h)], 3 * h + k - 1, device))
@@ -270,9 +269,9 @@
 
 
 def smoother_kernel(
-    live_ref, rows_ref, values_ref, pattern_ref, q_ref, near_ref, q_out, hh, hl, mean_acc, mean_ref, missed_ref,
-    m_ref, xb, rb, mh, mm, ml, gh, gl, vector_ref, r, w, u_ref, full, vecs,
-    send0, send1, send2, send3, parts0, parts1, parts2, parts3, send_sems, recv_sems,
+    live_ref, rows_ref, values_ref, pattern_ref, q_hbm, near_ref, q_out, hh, hl, mean_acc, mean_ref, missed_ref,
+    m_ref, xb, rb, mh, mm, ml, gh, gl, masked_ref, q_ref, q0, q1, q2, r, w, u_ref, full, vecs,
+    send0, send1, send2, send3, parts0, parts1, parts2, parts3, send_sems, recv_sems, local_sem,
 ):
     leaf, core = lax.axis_index("leaf"), lax.axis_index("blk")
     z, y, x = place(leaf)
@@ -284,7 +283,12 @@
             pl.semaphore_signal(barrier, inc=1, device_id=peer, device_id_type=MESH)
     pl.semaphore_signal(barrier, inc=1, device_id=(leaf, 1 - core), device_id_type=MESH)
 
-    m, vector_ref[...] = observe(live_ref, rows_ref, values_ref, pattern_ref, q_ref)
+    load_q = pltpu.make_async_copy(q_hbm, q_ref, local_sem)
+    load_q.start()
+    masked_ref[...] = observe(live_ref, rows_ref, pattern_ref)
+    gram = dot(masked_ref[...], masked_ref[...], ((0,), (0,)))
+    load_q.wait()
+    m = gram + q_ref[...]
     m_ref[...] = m
     bound = jnp.max(jnp.sum(jnp.abs(m), axis=0, keepdims=True)) * 1.00001
     invert(m_ref, xb, rb, mh, mm, ml, 1.0 / bound, 1.0 / 64.0, 4)
@@ -296,14 +300,16 @@
     def leaf_first():
         v, missed = inverse_whole(m_ref, xb, rb, mh, ml)
         gh[...], gl[...] = split(v)
-        w[0] = flagged(mm3(split(vector_ref[...]), (gh[...], gl[...])), 0.0, missed)
+        vector = mm3_row(jnp.broadcast_to(values_ref[...], (8, N)), masked_ref[...])
+        w[0] = flagged(mm3(split(vector), (gh[...], gl[...])), 0.0, missed)
         mean_acc[...] = w[0]
         m_ref[...] = v
         near_ref[...] = m_ref[:, pl.ds(pl.multiple_of(core * HALF, HALF), HALF)]
         r[...] = near_ref[...]
 
     def leaf_second():
-        hh[...], hl[...] = split(mm3((gh[...], gl[...]), split(q_ref[...])))
+        q0[...], q1[...], q2[...] = split3(q_ref[...])
+        hh[...], hl[...] = split(mm3((gh[...], gl[...]), (q0[...], q1[...])))
 
     def tier_first(n):
         def work():
@@ -334,7 +340,7 @@
             exchange(tier, *shared, tier_first(tier), tier_second(tier))
         total = full[tier].reshape(N, N)
         if tier == 0:
-            m_ref[...] = 5.0 * eye() - mm6(split3(total), split3(q_ref[...]))
+            m_ref[...] = 5.0 * eye() - mm6(split3(total), (q0[...], q1[...], q2[...]))
         else:
             m_ref[...] = 5.0 * eye() - total
         invert(m_ref, xb, rb, mh, mm, ml, 1.0 / 5.001, 0.1999, 2)
@@ -380,13 +386,13 @@
             matrix(N, HALF), matrix(N, HALF), matrix(dtype=BF16), matrix(dtype=BF16), matrix(8), matrix(8),
             jax.ShapeDtypeStruct((1,), F32),
         ),
-        in_specs=[SMEM_SPEC] + [VMEM_SPEC] * 4,
+        in_specs=[SMEM_SPEC] + [VMEM_SPEC] * 3 + [ANY_SPEC],
         out_specs=(VMEM_SPEC,) * 6 + (SMEM_SPEC,),
         scratch_shapes=[
-            square(F32), *[square(BF16)] * 7, vector, pltpu.VMEM((N, HALF), F32), pltpu.VMEM((4, 8, N), F32), vector,
+            square(F32), *[square(BF16)] * 8, square(F32), *[square(BF16)] * 3, pltpu.VMEM((N, HALF), F32), pltpu.VMEM((4, 8, N), F32), vector,
             pltpu.VMEM((4, 8, 4, 16, N), F32), pltpu.VMEM((4, 4, 8, N), F32),
             *[pltpu.VMEM(shape, F32) for shape in sends], *[pltpu.VMEM((4, *shape), F32) for shape in pieces],
-            pltpu.SemaphoreType.DMA((4, SEMS)), pltpu.SemaphoreType.DMA((4, SEMS)),
+            pltpu.SemaphoreType.DMA((4, SEMS)), pltpu.SemaphoreType.DMA((4, SEMS)), pltpu.SemaphoreType.DMA,
         ],
         compiler_params=pltpu.CompilerParams(vmem_limit_bytes=LIMIT, collective_id=0, has_side_effects=True),
     )(track_blocks, obs_rows, obs_values[None, :], pattern, process_info)
@@ -609,7 +615,9 @@
 
 
 def careful_leaf_kernel(live_ref, rows_ref, values_ref, pattern_ref, q_ref, m_ref, vector_ref):
-    m_ref[...], vector_ref[...] = observe(live_ref, rows_ref, values_ref, pattern_ref, q_ref)
+    masked = observe(live_ref, rows_ref, pattern_ref)
+    vector_ref[...] = mm3_row(jnp.broadcast_to(values_ref[...], (8, N)), masked)
+    m_ref[...] = dot(masked, masked, ((0,), (0,))) + q_ref[...]
 
 
 def careful(obs_rows, obs_values, track_blocks, pattern, process_info):

time: 110 us -> 108 us (0.982)
  Pallas kernels: 108 us -> 105 us
    pallas_call x1, Pallas kernels: 105 us -> 102 us  [smoother(): pl.pallas_call(smoother_kernel, out_shape=(matrix(N, HALF), matrix(N, HAL...]
where the time goes in v5:
time: 108 us; the launch traced here: 107 us
  Pallas kernels  105 us (97%)
  between operations  1.51 us (1%)
    pallas_call x1, Pallas kernels, smoother(): pl.pallas_call(smoother_kernel, out_shape=(matrix(N, HALF), matrix(N, HAL...  102 us
    pallas_call x1, Pallas kernels, last(): pl.pallas_call(last_kernel, out_shape=(matrix(N, HALF), matrix(1)), grid=...  3.27 us

profile of v5, /device:TPU:1, one launch (start us, length us, event | category | flops | bytes accessed | tf_op | source)
XLA Modules:
  0.0 107.5 jit_solution(12678921202112921509)
XLA Ops:
  0.6 0.0 copy-start.8
  0.6 0.0 copy-start.9
  1.3 102.2 %shard_map.68 = (f32[512,256]{1,0:T(8,128)}, f32[512,256]{1,0:T(8,128)}, bf16[512,512]{1,0:T(8,128)(2,1)}, bf16[512,512]{1,0:T(8,128)(2,1)}, f32[8,512]{1,0:T(8,128)}, /*index=5*/f32[8,512]{1,0:T(8,128)}, f32[1]{0:T(128)}) custom-call(s32[1]{0:T(128)S(6)} %copy.24.live_ref, bf16[512,512]{1,0:T(8,128)(2,1)} %rows_ref.1, f32[1,512]{1,0:T(1,128)} %bitcast.35, ...), custom_call_target="tpu_custom_call" | custom-call | tf_op jit(solution)/shard_map/pallas_call | solution.py:383
  103.5 3.3 %shard_map.69 = (f32[512,256]{1,0:T(8,128)}, f32[1,512]{1,0:T(1,128)}) custom-call(f32[512,256]{1,0:T(8,128)} %get-tuple-element.83.near_ref, f32[512,256]{1,0:T(8,128)} %get-tuple-element.84.q_ref, bf16[512,512]{1,0:T(8,128)(2,1)} %get-tuple-element.85.hh_ref, bf16[512,512]{1,0:T(8,128)(2,1)} %get-tuple-element.86.hl_ref, ...), custom_call_target="tpu_custom_call" | custom-call | tf_op jit(solution)/shard_map/pallas_call | solution.py:418
  106.7 0.0 copy-done.8
  106.8 0.0 copy-done.9
  106.8 0.6 while.20
Async XLA Ops:
  0.6 106.1 %copy-start.8 = (f32[512]{0:T(512)S(1)}, f32[512]{0:T(512)}, u32[]{:S(2)}) copy-start(f32[512]{0:T(512)} %param.10) | copy-start | bytes 6148
  0.6 106.1 %copy-start.9 = (s32[4,64]{1,0:T(4,128)S(1)}, s32[4,64]{1,0:T(4,128)}, u32[]{:S(2)}) copy-start(s32[4,64]{1,0:T(4,128)} %pattern_ref.1) | copy-start | bytes 3076
